TPU v7x, 32 devices: a whole 2x2x4 slice. The times are simulated.
32 devices in a mesh: groups: 2 (over x), lat: 16 (over z, y, core).
Axes of the slice: x: 2, y: 2, z: 4, core: 2. Of those that a mesh axis runs over, the one named last changes fastest.
Arguments:
- ocean_state: float32 [4, 16, 64, 384], P(None, None, ('groups', 'lat')), parts along dimension 2, may hold values from -4 to 4
- bottom: int32 [64, 384], P(('groups', 'lat')), parts along dimension 0, may hold values from 4 to 16
- tracers: float32 [16, 16, 768, 32], P(None, None, ('groups', 'lat')), parts along dimension 2, may hold values from -4 to 4
- land_sea: int32 [16, 768, 32], P(None, ('groups', 'lat')), parts along dimension 1, may hold values 0 or 1
- biome_id: int32 [768, 32], P(('groups', 'lat')), parts along dimension 0, may hold values from 0 to 3
- rate_table: float32 [4, 16, 16], replicated, may hold values from -1.5 to 1.5
Outputs:
- state_out: float32 [4, 16, 64, 384], P(None, None, ('groups', 'lat')), parts along dimension 2
- tracers_out: float32 [16, 16, 768, 32], P(None, None, ('groups', 'lat')), parts along dimension 2
There are 2 independent parts, one for each index of `groups`. A program takes and returns all parts, laid end to end along the dimension named above; an argument that names none is the same for every part. Nothing has to cross between parts.
All inputs are finite; a program needn't handle non-finite values. No bound on the sum of `land_sea` on one device may be relied on, other than what follows from the above.
Results may differ from a plain program's by a relative error of at most 0.00014.
Values sent between devices are 32-bit elements; how exact they have to be, the bound alone decides.
No kernel may reach another device: no remote copies, remote signals or barrier semaphores. Data moves between devices by JAX's collectives and lax.ppermute only.
A program may use at most 128 MiB of HBM per device.

v0:
```python
import jax
import jax.numpy as jnp
from jax import lax
from jax.experimental import pallas as pl
from jax.experimental.pallas import tpu as pltpu
from jax.sharding import PartitionSpec as P

STEPS = 2
SUB = 2


time_step = 0.1
viscosity = 0.1
heat_diff = 0.08
salt_diff = 0.06
therm_coef = 0.2
haline_coef = 0.15
gravity = 0.5
coriolis = 0.6
vert_ratio = 0.25
tracer_step = 0.1
tracer_diff = 0.1
water_atten = 0.04
chl_atten = 0.05
growth_rate = 0.8
heat_gain = 10.0


def extended(block, sides, width, periodic):
    for axis, dim in sides:
        count = lax.axis_size(axis)
        forward = [(i, i + 1) for i in range(count - 1)]
        if periodic:
            forward.append((count - 1, 0))
        backward = [(target, source) for source, target in forward]
        low = lax.ppermute(
            lax.slice_in_dim(block, block.shape[dim] - width, None, axis=dim), axis, forward
        )
        high = lax.ppermute(lax.slice_in_dim(block, 0, width, axis=dim), axis, backward)
        block = jnp.concatenate([low, block, high], axis=dim)
    return block


def laplace_rows(field):
    center = field[:, 1:-1, :]
    return (
        jnp.roll(center, 1, 2)
        + jnp.roll(center, -1, 2)
        + field[:, 2:, :]
        + field[:, :-2, :]
        - 4.0 * center
    )


def ocean_core(padded, wet_mask, lat_start, total_lat):
    speed_u, speed_v, temper, salty = (padded[0], padded[1], padded[2], padded[3])
    east_mid = speed_u[:, 1:-1, :]
    north_mid = speed_v[:, 1:-1, :]
    temp_mid = temper[:, 1:-1, :]
    salt_mid = salty[:, 1:-1, :]
    pressure = gravity * jnp.cumsum(haline_coef * salty - therm_coef * temper, axis=0)
    press_mid = pressure[:, 1:-1, :]
    row_index = (lat_start + jnp.arange(wet_mask.shape[1], dtype=jnp.int32)).astype(jnp.float32)
    spin_rate = (coriolis * (2.0 * (row_index + 0.5) / total_lat - 1.0))[None, :, None]
    slope_east = 0.5 * (jnp.roll(press_mid, -1, 2) - jnp.roll(press_mid, 1, 2))
    slope_north = 0.5 * (pressure[:, 2:, :] - pressure[:, :-2, :])
    new_u = wet_mask * (
        east_mid
        + time_step * (spin_rate * north_mid - slope_east + viscosity * laplace_rows(speed_u))
    )
    new_v = wet_mask * (
        north_mid
        + time_step * (-spin_rate * east_mid - slope_north + viscosity * laplace_rows(speed_v))
    )
    new_s = wet_mask * (salt_mid + time_step * salt_diff * laplace_rows(salty))
    part_t = temp_mid + time_step * heat_diff * laplace_rows(temper)
    spread = 0.5 * (jnp.roll(east_mid, -1, 2) - jnp.roll(east_mid, 1, 2)) + 0.5 * (
        speed_v[:, 2:, :] - speed_v[:, :-2, :]
    )
    rise_flux = -vert_ratio * jnp.flip(jnp.cumsum(jnp.flip(spread, 0), axis=0), 0)
    fluxes = jnp.stack([east_mid, north_mid, rise_flux])
    return (new_u, new_v, part_t, new_s, fluxes)


def light_field(plankton):
    chloro = jax.nn.softplus(plankton)
    attenuate = water_atten + chl_atten * chloro
    depth = jnp.cumsum(attenuate, axis=0) - attenuate
    row_index = jnp.arange(plankton.shape[-1], dtype=jnp.int32).astype(jnp.float32)
    place = 2.0 * (row_index + 0.5) / plankton.shape[-1] - 1.0
    surface = 1.0 - 0.5 * place * place
    top_light = surface * jnp.exp(-depth)
    return (chloro, top_light, top_light * (1.0 - jnp.exp(-attenuate)))


def tracer_core(tracer_ext, flux_ext, sea_mask, onehot, rate_table):
    center = tracer_ext[:, :, 1:-1, :]
    east_face = 0.5 * (flux_ext[0, :, :-1, :] + flux_ext[0, :, 1:, :])
    across = (
        jnp.maximum(east_face, 0.0) * tracer_ext[:, :, :-1, :]
        + jnp.minimum(east_face, 0.0) * tracer_ext[:, :, 1:, :]
    )
    div_east = across[:, :, 1:, :] - across[:, :, :-1, :]
    north_speed = flux_ext[1, :, 1:-1, :]
    north_face = 0.5 * (north_speed[:, :, :-1] + north_speed[:, :, 1:])
    along = (
        jnp.maximum(north_face, 0.0) * center[..., :-1]
        + jnp.minimum(north_face, 0.0) * center[..., 1:]
    )
    along = jnp.pad(along, ((0, 0), (0, 0), (0, 0), (1, 1)))
    div_north = along[..., 1:] - along[..., :-1]
    rise_face = flux_ext[2, 1:, 1:-1, :]
    upward = (
        jnp.maximum(rise_face, 0.0) * center[:, 1:] + jnp.minimum(rise_face, 0.0) * center[:, :-1]
    )
    upward = jnp.pad(upward, ((0, 0), (1, 1), (0, 0), (0, 0)))
    div_up = upward[:, :-1] - upward[:, 1:]
    side = jnp.pad(center, ((0, 0), (0, 0), (0, 0), (1, 1)))
    diffuse = (
        tracer_ext[:, :, 2:, :]
        + tracer_ext[:, :, :-2, :]
        + side[..., 2:]
        + side[..., :-2]
        - 4.0 * center
    )
    chloro, top_light, absorbed = light_field(center[0])
    nutrient = center[1] * center[1]
    uptake = growth_rate * top_light * chloro * nutrient / (1.0 + nutrient)
    rate_cell = jnp.einsum("bst,bij->stij", rate_table, onehot, precision=lax.Precision.HIGHEST)
    reaction = jnp.einsum("stij,tkij->skij", rate_cell, center, precision=lax.Precision.HIGHEST)
    reaction = reaction.at[0].add(uptake).at[1].add(-uptake)
    tendency = tracer_diff * diffuse + reaction - (div_east + div_north + div_up)
    return sea_mask[None] * (center + tracer_step * tendency)


def general_shards(ocean_state, bottom, tracers, land_sea, biome_id, rate_table):
    levels = ocean_state.shape[1]
    lat_rows = ocean_state.shape[2]
    lat_count = lax.axis_size("lat")
    total_lat = lat_rows * lat_count
    lat_start = lax.axis_index("lat") * lat_rows
    wet_mask = (jnp.arange(levels, dtype=jnp.int32)[:, None, None] < bottom[None]).astype(
        jnp.float32
    )
    sea_mask = land_sea.astype(jnp.float32)
    onehot = (
        biome_id[None] == jnp.arange(rate_table.shape[0], dtype=jnp.int32)[:, None, None]
    ).astype(jnp.float32)
    state = ocean_state
    tracer_now = tracers
    for cycle_index in range(STEPS):
        state = state * wet_mask[None]
        padded = extended(state, (("lat", 2),), 1, False)
        new_u, new_v, part_t, new_s, fluxes = ocean_core(padded, wet_mask, lat_start, total_lat)
        flux_t = lax.all_to_all(
            jnp.transpose(fluxes, (0, 1, 3, 2)), "lat", split_axis=2, concat_axis=3, tiled=True
        )
        tracer_now = tracer_now * sea_mask[None]
        flux_ext = extended(flux_t, (("lat", 2),), 1, True)
        for sub_index in range(SUB):
            tracer_ext = extended(tracer_now, (("lat", 2),), 1, True)
            tracer_now = tracer_core(tracer_ext, flux_ext, sea_mask, onehot, rate_table)
        heating = heat_gain * sea_mask * light_field(tracer_now[0])[2]
        heat_ocean = jnp.transpose(
            lax.all_to_all(heating, "lat", split_axis=2, concat_axis=1, tiled=True), (0, 2, 1)
        )
        new_t = wet_mask * (part_t + time_step * heat_ocean)
        state = jnp.stack([new_u, new_v, new_t, new_s])
    return (state, tracer_now)


HALO = STEPS * SUB
LANES = 128
TILE = 8
FIELDS = 4


def fits(ocean_state, tracers, rate_table, lat_count):
    _, levels, lat_rows, total_lon = ocean_state.shape
    species, _, columns, total_lat = tracers.shape
    return (
        lat_rows == 2
        and HALO == TILE // 2
        and lat_rows * lat_count == total_lat
        and columns * lat_count == total_lon
        and columns % TILE == 0
        and LANES % total_lat == 0
        and (columns + 2 * HALO) * total_lat == TILE * LANES
        and 2 * FIELDS * levels == LANES
        and levels <= columns + HALO
        and 2 * columns + 3 * HALO <= FIELDS * levels
        and species == 2 * TILE
        and levels % (LANES // total_lat) == 0
    )


def rows_of(shape=(TILE, LANES)):
    return lax.broadcasted_iota(jnp.int32, shape, 0)


def lanes_of(shape=(TILE, LANES)):
    return lax.broadcasted_iota(jnp.int32, shape, 1)


def spin(block, amount, axis):
    size = block.shape[axis]
    amount = amount % size
    return block if amount == 0 else pltpu.roll(block, amount, axis)


def swap_halves(block):
    low_row, low_lane = rows_of() < TILE // 2, lanes_of() < LANES // 2
    other = spin(spin(block, LANES // 2, 1), TILE // 2, 0)
    return jnp.where(low_row == low_lane, block, other)


def pack_ocean(ocean_ref, bottom_ref, out_ref, flat, depth):
    fields, levels, lat_rows, total_lon = ocean_ref.shape
    half = fields * levels
    count = out_ref.shape[0] // (4 * TILE)
    columns = total_lon // count
    own = columns // TILE
    for index in range(half):
        field, level = divmod(index, levels)
        for row in range(lat_rows):
            flat[row * half + index : row * half + index + 1, :] = ocean_ref[field, level, row : row + 1, :]
    turned = flat[...].T
    tiles = [turned[TILE * i : TILE * (i + 1), :] for i in range(total_lon // TILE)]
    swapped = [swap_halves(t) for t in tiles]
    depth[...] = jnp.zeros(depth.shape, jnp.float32)
    depth[3:4, :] = bottom_ref[0:1, :].astype(jnp.float32)
    depth[7:8, :] = bottom_ref[1:2, :].astype(jnp.float32)
    line = depth[...]
    row, lane = rows_of(), lanes_of()
    width = columns + 2 * HALO
    window = (row % 4 == 3) & (lane >= width - HALO) & (lane < 2 * width - HALO)
    for target in range(count):
        for q in range(own):
            out_ref[pl.ds((target * (own + 1) + q) * TILE, TILE), :] = swapped[target * own + q]
        east = tiles[(target * own + own) % len(tiles)]
        west = tiles[target * own - 1]
        edge = swap_halves(jnp.where(row < HALO, east, west))
        level_line = spin(line, width - target * columns, 1)[:, :LANES]
        out_ref[pl.ds((target * (own + 1) + own) * TILE, TILE), :] = jnp.where(window, level_line, edge)


def pack_edges(tracer_ref, sea_ref, biome_ref, west_ref, east_ref):
    species, levels, columns, total_lat = tracer_ref.shape
    blocks = LANES // total_lat
    groups = levels // blocks
    low = rows_of((TILE, total_lat)) < HALO
    last = columns - TILE
    for group in range(groups):
        wet = [
            jnp.where(low, sea_ref[group * blocks + b, 0:TILE, :], sea_ref[group * blocks + b, last:columns, :]).astype(
                jnp.float32
            )
            for b in range(blocks)
        ]
        joined = jnp.concatenate(wet, axis=1)
        start = species * groups * HALO + group * HALO
        west_ref[start : start + HALO, :] = joined[:HALO, :]
        east_ref[start : start + HALO, :] = joined[HALO:, :]
        for kind in range(species):
            parts = [
                jnp.where(
                    low,
                    tracer_ref[kind, group * blocks + b, 0:TILE, :],
                    tracer_ref[kind, group * blocks + b, last:columns, :],
                )
                for b in range(blocks)
            ]
            both = jnp.concatenate(parts, axis=1) * joined
            start = (kind * groups + group) * HALO
            west_ref[start : start + HALO, :] = both[:HALO, :]
            east_ref[start : start + HALO, :] = both[HALO:, :]
    biome = jnp.where(low, biome_ref[0:TILE, :], biome_ref[last:columns, :]).astype(jnp.float32)
    biome = jnp.concatenate([biome] * blocks, axis=1)
    start = (species + 1) * groups * HALO
    west_ref[start : start + 2 * HALO, :] = biome
    east_ref[start : start + 2 * HALO, :] = spin(biome, HALO, 0)


def light(plankton, surface):
    result = []
    depth = jnp.zeros(surface.shape, jnp.float32)
    for value in plankton:
        chloro = jnp.maximum(value, 0.0) + jnp.log1p(jnp.exp(-jnp.abs(value)))
        attenuate = water_atten + chl_atten * chloro
        result.append((chloro, surface * jnp.exp(-depth), attenuate))
        depth = depth + attenuate
    return result


def surface_light(total_lat):
    row_index = (lanes_of() % total_lat).astype(jnp.float32)
    place = 2.0 * (row_index + 0.5) / total_lat - 1.0
    return 1.0 - 0.5 * place * place


def planes_of(ref, kind, levels, species, base=0):
    return [ref[pl.ds(base + level * TILE * species + kind, TILE, stride=species), :] for level in range(levels)]


def put_growth(growth_ref, tracer_ref, levels, species, total_lat, base=0):
    lit = light(planes_of(tracer_ref, 0, levels, species, base), surface_light(total_lat))
    food = planes_of(tracer_ref, 1, levels, species, base)
    for level, (chloro, top_light, _) in enumerate(lit):
        nutrient = food[level] * food[level]
        uptake = growth_rate * top_light * chloro * nutrient / (1.0 + nutrient)
        growth_ref[level * TILE : (level + 1) * TILE, :] = tracer_step * uptake
    return lit


def spread_row(ref, index):
    return ref[pl.ds(index, TILE, stride=0), :]


def reaction(source_ref, base, rate_ref, growth_ref, row, levels, species):
    sums = [[None, None] for _ in levels]
    for kind in range(species):
        rates = [
            rate_ref[pl.ds((row * species + kind) * species + TILE * part, TILE), :] for part in range(2)
        ]
        for place, level in enumerate(levels):
            value = spread_row(source_ref, base + (level * TILE + row) * species + kind)
            for part in range(2):
                term = rates[part] * value
                sums[place][part] = term if sums[place][part] is None else sums[place][part] + term
    index = rows_of()
    sign = jnp.where(index == 0, 1.0, jnp.where(index == 1, -1.0, 0.0))
    for place, level in enumerate(levels):
        sums[place][0] = sums[place][0] + sign * spread_row(growth_ref, level * TILE + row)
    return sums


def prepare(tracer_ref, sea_ref, biome_ref, rate_table_ref, from_west, from_east, now_ref, wet_ref, rate_ref, first_ref, growth, rate_columns):
    species, levels, columns, total_lat = tracer_ref.shape
    kinds = rate_table_ref.shape[0]
    blocks = LANES // total_lat
    groups = levels // blocks
    own = columns // TILE

    def halo(start):
        return jnp.concatenate([from_east[start : start + HALO, :], from_west[start : start + HALO, :]], axis=0)

    def plane(parts, edge, block):
        return jnp.concatenate(parts + [edge[:, block * total_lat : (block + 1) * total_lat]], axis=1)

    for group in range(groups):
        edge = halo((species * groups + group) * HALO)
        for block in range(blocks):
            level = group * blocks + block
            parts = [sea_ref[level, TILE * q : TILE * (q + 1), :].astype(jnp.float32) for q in range(own)]
            wet_ref[level * TILE : (level + 1) * TILE, :] = plane(parts, edge, block)
    for kind in range(species):
        for group in range(groups):
            edge = halo((kind * groups + group) * HALO)
            for block in range(blocks):
                level = group * blocks + block
                parts = [tracer_ref[kind, level, TILE * q : TILE * (q + 1), :] for q in range(own)]
                whole = plane(parts, edge, block) * wet_ref[level * TILE : (level + 1) * TILE, :]
                now_ref[pl.ds(level * TILE * species + kind, TILE, stride=species), :] = whole
    start = (species + 1) * groups * HALO
    parts = [biome_ref[TILE * q : TILE * (q + 1), :].astype(jnp.float32) for q in range(own)]
    biome = plane(parts, halo(start), 0)
    for b in range(kinds):
        for kind in range(species):
            for part in range(2):
                column = rate_table_ref[b, TILE * part : TILE * (part + 1), kind : kind + 1]
                rate_columns[pl.ds(((b * species + kind) * 2 + part) * TILE, TILE), :] = tracer_step * jnp.broadcast_to(column, (TILE, LANES))
    for row in range(TILE):
        here = jnp.broadcast_to(biome[row : row + 1, :], (TILE, LANES))
        chosen = [here == float(b) for b in range(kinds)]
        for kind in range(species):
            for part in range(2):
                rate = jnp.zeros((TILE, LANES), jnp.float32)
                for b in range(kinds):
                    rate = jnp.where(chosen[b], rate_columns[pl.ds(((b * species + kind) * 2 + part) * TILE, TILE), :], rate)
                rate_ref[pl.ds((row * species + kind) * species + TILE * part, TILE), :] = rate
    put_growth(growth, now_ref, levels, species, total_lat)

    def react(group, carry):
        near = [group * 4 + i for i in range(4)]
        for row in range(TILE):
            for level, sums in zip(near, reaction(now_ref, 0, rate_ref, growth, row, near, species), strict=True):
                for part in range(2):
                    first_ref[pl.ds((level * TILE + row) * species + TILE * part, TILE), :] = sums[part]
        return carry

    lax.fori_loop(0, levels // 4, react, 0)


def advance(received, now_ref, wet_ref, rate_ref, first_ref, sent, last_ref, work, ocean, coef, tracer, growth, sizes):
    levels, species, total_lat, columns = sizes
    count = total_lat // 2
    own = columns // TILE
    half = FIELDS * levels
    row, lane = rows_of(), lanes_of()
    lat = lane % total_lat
    width = columns + 2 * HALO

    for r_low in range(4):
        for q in range(own + 1):
            for j in range(2):
                work[pl.ds(r_low * LANES + q * total_lat + j, count, stride=2), :] = received[
                    pl.ds(q * TILE + j * 4 + r_low, count, stride=(own + 1) * TILE), :
                ]
    turned = None
    for r_low in range(4):
        turned = work[r_low * LANES : (r_low + 1) * LANES, :].T
        for r_high in range(2):
            ocean[pl.ds(r_high * 4 + r_low, half, stride=TILE), :] = turned[r_high * half : (r_high + 1) * half, :]
    floors = [turned[width + TILE * q : width + TILE * (q + 1), :] for q in range(own)]
    floors.append(
        jnp.where(row < HALO, turned[width + columns : width + columns + TILE, :], turned[width - TILE : width, :])
    )
    floor = floors[own]
    for q in range(own):
        floor = jnp.where(lane // total_lat == q, spin(floors[q], (q - own) * total_lat, 1), floor)
    wet = [(float(level) < floor).astype(jnp.float32) for level in range(levels)]
    sea = [wet_ref[level * TILE : (level + 1) * TILE, :] for level in range(levels)]

    def read(field):
        return [ocean[(field * levels + k) * TILE : (field * levels + k + 1) * TILE, :] for k in range(levels)]

    def write(field, values):
        for k in range(levels):
            ocean[(field * levels + k) * TILE : (field * levels + k + 1) * TILE, :] = values[k]

    def east(x):
        y = spin(x, -1, 0)
        return jnp.where(row == TILE - 1, spin(y, -total_lat, 1), y)

    def west(x):
        y = spin(x, 1, 0)
        return jnp.where(row == 0, spin(y, total_lat, 1), y)

    def north(x):
        return jnp.where(lat == total_lat - 1, 0.0, spin(x, -1, 1))

    def south(x):
        return jnp.where(lat == 0, 0.0, spin(x, 1, 1))

    spin_rate = coriolis * (2.0 * (lat.astype(jnp.float32) + 0.5) / total_lat - 1.0)
    plane = levels * TILE

    def dynamics(step):
        speed_u, speed_v, temper, salty = read(0), read(1), read(2), read(3)
        spread, new_u, new_v = [], [], []
        pressure = None
        for k in range(levels):
            u, v = speed_u[k], speed_v[k]
            part = gravity * (haline_coef * salty[k] - therm_coef * temper[k])
            pressure = part if pressure is None else pressure + part
            slope_east = 0.5 * (east(pressure) - west(pressure))
            slope_north = 0.5 * (north(pressure) - south(pressure))
            u_east, u_west, v_north, v_south = east(u), west(u), north(v), south(v)
            lap_u = u_east + u_west + north(u) + south(u) - 4.0 * u
            lap_v = east(v) + west(v) + v_north + v_south - 4.0 * v
            new_u.append(wet[k] * (u + time_step * (spin_rate * v - slope_east + viscosity * lap_u)))
            new_v.append(wet[k] * (v + time_step * (-spin_rate * u - slope_north + viscosity * lap_v)))
            spread.append(0.5 * (u_east - u_west) + 0.5 * (v_north - v_south))
            face_east = 0.5 * (u + u_east)
            face_north = jnp.where(lat == total_lat - 1, 0.0, 0.5 * (v + v_north))
            up_east, down_east = jnp.maximum(face_east, 0.0), jnp.minimum(face_east, 0.0)
            up_north, down_north = jnp.maximum(face_north, 0.0), jnp.minimum(face_north, 0.0)
            mask = tracer_step * sea[k]
            at = step * 7 * plane + k * TILE
            coef[pl.ds(at + plane, TILE), :] = mask * (tracer_diff - down_east)
            coef[pl.ds(at + 2 * plane, TILE), :] = mask * (tracer_diff + west(up_east))
            coef[pl.ds(at + 3 * plane, TILE), :] = jnp.where(
                lat == total_lat - 1, 0.0, mask * (tracer_diff - down_north)
            )
            coef[pl.ds(at + 4 * plane, TILE), :] = jnp.where(lat == 0, 0.0, mask * (tracer_diff + south(up_north)))
            coef[pl.ds(at, TILE), :] = -4.0 * tracer_diff - up_east + west(down_east) - up_north + south(down_north)
        total = jnp.zeros((TILE, LANES), jnp.float32)
        below_up, below_down = total, total
        for k in reversed(range(levels)):
            total = total + spread[k]
            rise = -vert_ratio * total if k > 0 else jnp.zeros((TILE, LANES), jnp.float32)
            up, down = jnp.maximum(rise, 0.0), jnp.minimum(rise, 0.0)
            mask = tracer_step * sea[k]
            at = step * 7 * plane + k * TILE
            coef[pl.ds(at, TILE), :] = sea[k] + mask * (coef[pl.ds(at, TILE), :] - up + below_down)
            coef[pl.ds(at + 5 * plane, TILE), :] = -mask * down
            coef[pl.ds(at + 6 * plane, TILE), :] = mask * below_up
            below_up, below_down = up, down
        for field, values, rate in ((2, temper, heat_diff), (3, salty, salt_diff)):
            fresh = []
            for k in range(levels):
                x = values[k]
                lap = east(x) + west(x) + north(x) + south(x) - 4.0 * x
                y = x + time_step * rate * lap
                fresh.append(wet[k] * y if field == 3 else y)
            write(field, fresh)
        write(0, new_u)
        write(1, new_v)

    def substep(step, source, base, target, target_base, ready):
        start = step * 7 * plane

        def body(group, carry):
            near = [group * 4 + i for i in range(4)]
            for r in range(TILE):
                if ready is None:
                    sums = reaction(source, base, rate_ref, growth, r, near, species)
                for place, level in enumerate(near):
                    cell = level * TILE + r
                    weight = [spread_row(coef, start + i * plane + cell) for i in range(7)]
                    mask = spread_row(wet_ref, cell)
                    above = jnp.maximum(level - 1, 0) * TILE + r
                    under = jnp.minimum(level + 1, levels - 1) * TILE + r
                    for part in range(2):

                        def take(index, part=part):
                            return source[pl.ds(base + index * species + TILE * part, TILE), :]

                        x = take(cell)
                        x_east = take(cell + 1) if r < TILE - 1 else spin(take(cell - r), -total_lat, 1)
                        x_west = take(cell - 1) if r > 0 else spin(take(cell + TILE - 1), total_lat, 1)
                        if ready is None:
                            change = sums[place][part]
                        else:
                            change = ready[pl.ds(cell * species + TILE * part, TILE), :]
                        value = (
                            (weight[0] * x + weight[1] * x_east)
                            + (weight[2] * x_west + weight[3] * spin(x, -1, 1))
                            + (weight[4] * spin(x, 1, 1) + weight[5] * take(above))
                            + (weight[6] * take(under) + mask * change)
                        )
                        target[pl.ds(target_base + cell * species + TILE * part, TILE), :] = value
            return carry

        lax.fori_loop(0, levels // 4, body, 0)

    for field in range(FIELDS):
        write(field, [wet[k] * x for k, x in enumerate(read(field))])
    size = levels * TILE * species
    source, base = now_ref, 0
    lit = None
    for step in range(STEPS):
        dynamics(step)
        for sub in range(SUB):
            last = step == STEPS - 1 and sub == SUB - 1
            first = step == 0 and sub == 0
            target, target_base = (last_ref, 0) if last else (tracer, ((step * SUB + sub) % 2) * size)
            if not first:
                put_growth(growth, source, levels, species, total_lat, base)
            substep(step, source, base, target, target_base, first_ref if first else None)
            source, base = target, target_base
        lit = light(planes_of(source, 0, levels, species, base), surface_light(total_lat))
        warm = []
        for k, x in enumerate(read(2)):
            _, top_light, attenuate = lit[k]
            heating = heat_gain * sea[k] * (top_light * (1.0 - jnp.exp(-attenuate)))
            warm.append(wet[k] * (x + time_step * heating))
        write(2, warm)

    for r_low in range(4):
        both = jnp.concatenate(
            [ocean[pl.ds(r_high * 4 + r_low, half, stride=TILE), :] for r_high in range(2)], axis=0
        )
        work[r_low * LANES : (r_low + 1) * LANES, :] = both.T
        for q in range(own):
            for j in range(2):
                sent[pl.ds(q * TILE + j * 4 + r_low, count, stride=own * TILE), :] = work[
                    pl.ds(r_low * LANES + q * total_lat + j, count, stride=2), :
                ]


def unpack_tracers(last_ref, out_ref):
    species, levels, columns, total_lat = out_ref.shape
    for level in range(levels):
        for kind in range(species):
            whole = last_ref[pl.ds(level * TILE * species + kind, TILE, stride=species), :]
            for q in range(columns // TILE):
                out_ref[kind, level, TILE * q : TILE * (q + 1), :] = whole[:, q * total_lat : (q + 1) * total_lat]


def unpack_ocean(received, out_ref, turned, flat):
    fields, levels, lat_rows, total_lon = out_ref.shape
    half = fields * levels
    for i in range(total_lon // TILE):
        turned[TILE * i : TILE * (i + 1), :] = swap_halves(received[TILE * i : TILE * (i + 1), :])
    flat[...] = turned[...].T
    for index in range(half):
        field, level = divmod(index, levels)
        for row in range(lat_rows):
            out_ref[field, level, row : row + 1, :] = flat[row * half + index : row * half + index + 1, :]


def grids(*shapes):
    return [pltpu.VMEM(shape, jnp.float32) for shape in shapes]


def real(*shape):
    return jax.ShapeDtypeStruct(shape, jnp.float32)


def shards(ocean_state, bottom, tracers, land_sea, biome_id, rate_table):
    count = lax.axis_size("lat")
    if not fits(ocean_state, tracers, rate_table, count):
        return general_shards(ocean_state, bottom, tracers, land_sea, biome_id, rate_table)
    _, levels, _, total_lon = ocean_state.shape
    species, _, columns, total_lat = tracers.shape
    cells = levels * TILE
    size = cells * species
    own = columns // TILE

    packed = pl.pallas_call(
        pack_ocean,
        out_shape=real(count * (own + 1) * TILE, LANES),
        scratch_shapes=grids((LANES, total_lon), (TILE, total_lon)),
        name="pack_ocean",
    )(ocean_state, bottom)
    received = lax.all_to_all(
        packed.reshape(count, (own + 1) * TILE, LANES), "lat", split_axis=0, concat_axis=0, tiled=True
    ).reshape(packed.shape)

    edge_rows = (species + 1) * (levels * total_lat // LANES) * HALO + 2 * HALO
    to_west, to_east = pl.pallas_call(
        pack_edges, out_shape=[real(edge_rows, LANES)] * 2, name="pack_edges"
    )(tracers, land_sea, biome_id)
    forward = [(i, (i + 1) % count) for i in range(count)]
    from_west = lax.ppermute(to_east, "lat", forward)
    from_east = lax.ppermute(to_west, "lat", [(b, a) for a, b in forward])

    now, wet, rates, first = pl.pallas_call(
        prepare,
        out_shape=[real(size, LANES), real(cells, LANES), real(TILE * species * species, LANES), real(size, LANES)],
        scratch_shapes=grids((cells, LANES), (rate_table.shape[0] * species * 2 * TILE, LANES)),
        name="prepare",
    )(tracers, land_sea, biome_id, rate_table, from_west, from_east)

    def run(*refs):
        advance(*refs, (levels, species, total_lat, columns))

    sent, last = pl.pallas_call(
        run,
        out_shape=[real(count * own * TILE, LANES), real(size, LANES)],
        scratch_shapes=grids(
            (4 * LANES, LANES),
            (FIELDS * cells, LANES),
            (STEPS * 7 * cells, LANES),
            (2 * size, LANES),
            (cells, LANES),
        ),
        name="advance",
    )(received, now, wet, rates, first)
    back = lax.all_to_all(
        sent.reshape(count, own * TILE, LANES), "lat", split_axis=0, concat_axis=0, tiled=True
    ).reshape(sent.shape)
    tracers_out = pl.pallas_call(
        unpack_tracers, out_shape=jax.ShapeDtypeStruct(tracers.shape, jnp.float32), name="unpack_tracers"
    )(last)
    state_out = pl.pallas_call(
        unpack_ocean,
        out_shape=jax.ShapeDtypeStruct(ocean_state.shape, jnp.float32),
        scratch_shapes=grids((total_lon, LANES), (LANES, total_lon)),
        name="unpack_ocean",
    )(back)
    return (state_out, tracers_out)


def solution(mesh):
    in_specs = (
        P(None, None, ("groups", "lat"), None),
        P(("groups", "lat"), None),
        P(None, None, ("groups", "lat"), None),
        P(None, ("groups", "lat"), None),
        P(("groups", "lat"), None),
        P(),
    )
    out_specs = (P(None, None, ("groups", "lat"), None), P(None, None, ("groups", "lat"), None))
    return jax.shard_map(shards, mesh=mesh, in_specs=in_specs, out_specs=out_specs, check_vma=False)
```

profile of v0, /device:TPU:0, one launch (start us, length us, event | category | flops | bytes accessed | tf_op | source)
XLA Modules:
  0.0 58.0 jit_solution(4221277368653702422)
XLA Ops:
  0.6 1.9 %pack_ocean.1 = f32[512,128]{1,0:T(8,128)} custom-call(f32[4,16,2,384]{3,2,1,0:T(2,128)} %ocean_ref.1, s32[2,384]{1,0:T(2,128)} %bottom_ref.1), custom_call_target="tpu_custom_call" | custom-call | tf_op jit(solution)/shard_map/pack_ocean/pallas_call | solution.py:611
  2.6 7.4 %all-to-all-start = ((f32[16,32,128]{2,1,0:T(8,128)}), f32[16,32,128]{2,1,0:T(8,128)S(1)}, u32[]{:S(2)}, u32[]{:S(2)}) async-start(f32[16,32,128]{2,1,0:T(8,128)} %bitcast.4), calls=%async_computation | async-start | bytes 524288 | tf_op jit(solution)/shard_map/all_to_all | solution.py:617
  10.0 3.0 %pack_edges.1 = (f32[280,128]{1,0:T(8,128)}, f32[280,128]{1,0:T(8,128)}) custom-call(f32[16,16,24,32]{3,2,1,0:T(8,128)} %tracer_ref.3, s32[16,24,32]{2,1,0:T(8,128)} %sea_ref.3, s32[24,32]{1,0:T(8,128)} %biome_ref.3), custom_call_target="tpu_custom_call" | custom-call | tf_op jit(solution)/shard_map/pack_edges/pallas_call | solution.py:622
  13.0 0.4 collective-permute-start
  13.4 4.0 %collective-permute-start.1 = (f32[280,128]{1,0:T(8,128)}, f32[280,128]{1,0:T(8,128)S(1)}, u32[]{:S(2)}, u32[]{:S(2)}) collective-permute-start(f32[280,128]{1,0:T(8,128)} %get-tuple-element.11), channel_id=1, source_target_pairs={{1,0},{2,1},{3,2},{4,3},{5,4},{6,5},{7,6},{8,7},{9,8},{10,9},{11,1... | collective-permute-start | bytes 430088 | tf_op jit(solution)/shard_map/ppermute | solution.py:627
  17.4 4.1 %collective-permute-done.from_west = f32[280,128]{1,0:T(8,128)S(1)} collective-permute-done((f32[280,128]{1,0:T(8,128)}, f32[280,128]{1,0:T(8,128)S(1)}, u32[]{:S(2)}, u32[]{:S(2)}) %collective-permute-start) | collective-permute-done | bytes 143392 | tf_op jit(solution)/shard_map/ppermute | solution.py:626
  21.5 0.0 copy-start.2
  21.6 0.0 collective-permute-done.1.from_east
  21.6 0.6 %copy-done.2 = f32[280,128]{1,0:T(8,128)} copy-done((f32[280,128]{1,0:T(8,128)}, f32[280,128]{1,0:T(8,128)S(1)}, u32[]{:S(2)}) %copy-start.2) | copy-done | bytes 143384
  22.2 0.0 copy-start.3
  22.2 0.7 %copy-done.3 = f32[280,128]{1,0:T(8,128)} copy-done((f32[280,128]{1,0:T(8,128)}, f32[280,128]{1,0:T(8,128)S(1)}, u32[]{:S(2)}) %copy-start.3) | copy-done | bytes 143384
  22.9 6.0 %prepare.1 = (f32[2048,128]{1,0:T(8,128)}, f32[128,128]{1,0:T(8,128)}, f32[2048,128]{1,0:T(8,128)}, f32[2048,128]{1,0:T(8,128)}) custom-call(f32[16,16,24,32]{3,2,1,0:T(8,128)} %tracer_ref.3, s32[16,24,32]{2,1,0:T(8,128)} %sea_ref.3, s32[24,32]{1,0:T(8,128)} %biome_ref.3, f32[4,16,16]{2,1,0:T(8,128)} %rate_table_ref.1, f32[280,128]{1,0:T(8,128)} %copy-done.2, ...), custom_call_target="tpu_custom_call" | custom-call | tf_op jit(solution)/shard_map/prepare/pallas_call | solution.py:629
  28.9 0.0 all-to-all-done
  28.9 0.0 copy-start
  28.9 0.7 %copy-done = f32[16,32,128]{2,1,0:T(8,128)} copy-done((f32[16,32,128]{2,1,0:T(8,128)}, f32[16,32,128]{2,1,0:T(8,128)S(1)}, u32[]{:S(2)}) %copy-start) | copy-done | bytes 262168
  29.6 12.9 %advance.1 = (f32[384,128]{1,0:T(8,128)}, f32[2048,128]{1,0:T(8,128)}) custom-call(f32[512,128]{1,0:T(8,128)} %bitcast.5, f32[2048,128]{1,0:T(8,128)} %get-tuple-element.12.refs_1_, f32[128,128]{1,0:T(8,128)} %get-tuple-element.13.refs_2_, f32[2048,128]{1,0:T(8,128)} %get-tuple-element.14.refs_3_, f32[2048,128]{1,0:T(8,128)} %get-tuple-element.15.refs_4_), custom_call_target="tpu_custom_call" | custom-call | tf_op jit(solution)/shard_map/advance/pallas_call | solution.py:639
  42.5 4.1 %all-to-all-start.1 = ((f32[16,24,128]{2,1,0:T(8,128)}), f32[16,24,128]{2,1,0:T(8,128)S(1)}, u32[]{:S(2)}, u32[]{:S(2)}) async-start(f32[16,24,128]{2,1,0:T(8,128)} %bitcast.7), calls=%async_computation.1 | async-start | bytes 393216 | tf_op jit(solution)/shard_map/all_to_all | solution.py:651
  46.5 3.5 %unpack_tracers.1 = f32[16,16,24,32]{3,2,1,0:T(8,128)} custom-call(f32[2048,128]{1,0:T(8,128)} %get-tuple-element.17.last_ref), custom_call_target="tpu_custom_call" | custom-call | tf_op jit(solution)/shard_map/unpack_tracers/pallas_call | solution.py:654
  50.0 5.5 %all-to-all-done.1 = f32[16,24,128]{2,1,0:T(8,128)S(1)} async-done(((f32[16,24,128]{2,1,0:T(8,128)}), f32[16,24,128]{2,1,0:T(8,128)S(1)}, u32[]{:S(2)}, u32[]{:S(2)}) %all-to-all-start.1) | async-done | bytes 196640 | tf_op jit(solution)/shard_map/all_to_all | solution.py:651
  55.5 0.0 copy-start.1
  55.5 0.7 %copy-done.1 = f32[16,24,128]{2,1,0:T(8,128)} copy-done((f32[16,24,128]{2,1,0:T(8,128)}, f32[16,24,128]{2,1,0:T(8,128)S(1)}, u32[]{:S(2)}) %copy-start.1) | copy-done | bytes 196632
  56.2 1.8 %unpack_ocean.1 = f32[4,16,2,384]{3,2,1,0:T(2,128)} custom-call(f32[384,128]{1,0:T(8,128)} %bitcast.6), custom_call_target="tpu_custom_call" | custom-call | tf_op jit(solution)/shard_map/unpack_ocean/pallas_call | solution.py:657
Async XLA Ops:
  2.6 26.3 %all-to-all-start = ((f32[16,32,128]{2,1,0:T(8,128)}), f32[16,32,128]{2,1,0:T(8,128)S(1)}, u32[]{:S(2)}, u32[]{:S(2)}) async-start(f32[16,32,128]{2,1,0:T(8,128)} %bitcast.4), calls=%async_computation | async-start | bytes 524288 | tf_op jit(solution)/shard_map/all_to_all | solution.py:617
  13.0 8.5 %collective-permute-start = (f32[280,128]{1,0:T(8,128)}, f32[280,128]{1,0:T(8,128)S(1)}, u32[]{:S(2)}, u32[]{:S(2)}) collective-permute-start(f32[280,128]{1,0:T(8,128)} %get-tuple-element.10), channel_id=1, source_target_pairs={{0,1},{1,2},{2,3},{3,4},{4,5},{5,6},{6,7},{7,8},{8,9},{9,10},{10,1... | collective-permute-start | bytes 430088 | tf_op jit(solution)/shard_map/ppermute | solution.py:626
  13.4 8.1 %collective-permute-start.1 = (f32[280,128]{1,0:T(8,128)}, f32[280,128]{1,0:T(8,128)S(1)}, u32[]{:S(2)}, u32[]{:S(2)}) collective-permute-start(f32[280,128]{1,0:T(8,128)} %get-tuple-element.11), channel_id=1, source_target_pairs={{1,0},{2,1},{3,2},{4,3},{5,4},{6,5},{7,6},{8,7},{9,8},{10,9},{11,1... | collective-permute-start | bytes 430088 | tf_op jit(solution)/shard_map/ppermute | solution.py:627
  21.5 0.6 %copy-start.2 = (f32[280,128]{1,0:T(8,128)}, f32[280,128]{1,0:T(8,128)S(1)}, u32[]{:S(2)}) copy-start(f32[280,128]{1,0:T(8,128)S(1)} %collective-permute-done.from_west) | copy-start | bytes 430084
  22.2 0.7 %copy-start.3 = (f32[280,128]{1,0:T(8,128)}, f32[280,128]{1,0:T(8,128)S(1)}, u32[]{:S(2)}) copy-start(f32[280,128]{1,0:T(8,128)S(1)} %collective-permute-done.1.from_east) | copy-start | bytes 430084
  28.9 0.7 %copy-start = (f32[16,32,128]{2,1,0:T(8,128)}, f32[16,32,128]{2,1,0:T(8,128)S(1)}, u32[]{:S(2)}) copy-start(f32[16,32,128]{2,1,0:T(8,128)S(1)} %all-to-all-done) | copy-start | bytes 786436
  42.5 13.0 %all-to-all-start.1 = ((f32[16,24,128]{2,1,0:T(8,128)}), f32[16,24,128]{2,1,0:T(8,128)S(1)}, u32[]{:S(2)}, u32[]{:S(2)}) async-start(f32[16,24,128]{2,1,0:T(8,128)} %bitcast.7), calls=%async_computation.1 | async-start | bytes 393216 | tf_op jit(solution)/shard_map/all_to_all | solution.py:651
  55.5 0.7 %copy-start.1 = (f32[16,24,128]{2,1,0:T(8,128)}, f32[16,24,128]{2,1,0:T(8,128)S(1)}, u32[]{:S(2)}) copy-start(f32[16,24,128]{2,1,0:T(8,128)S(1)} %all-to-all-done.1) | copy-start | bytes 589828
where the time goes:
time: 58.4 us; the launch traced here: 58 us
  Pallas kernels  29.2 us (50%)
  starting transfers between devices  15.9 us (27%)
  waiting for transfers between devices  9.56 us (16%)
  local copies, waits for them, and re-layouts  2.69 us (5%)
  between operations  0.66 us (1%)
    pallas_call x1, Pallas kernels, shards(): pl.pallas_call(run, out_shape=[real(count * own * TILE, LANES), real(size...  12.9 us
    all_to_all x1, starting transfers between devices, shards(): lax.all_to_all(packed.reshape(count, (own + 1) * TILE, LANES), 'lat', spl...  7.41 us
    pallas_call x1, Pallas kernels, shards(): pl.pallas_call(prepare, out_shape=[real(size, LANES), real(cells, LANES),...  6 us
    all_to_all x1, waiting for transfers between devices, shards(): lax.all_to_all(sent.reshape(count, own * TILE, LANES), 'lat', split_axis=...  5.45 us
    ppermute x1, waiting for transfers between devices, shards(): from_west = lax.ppermute(to_east, 'lat', forward)  4.1 us
    all_to_all x1, starting transfers between devices, shards(): lax.all_to_all(sent.reshape(count, own * TILE, LANES), 'lat', split_axis=...  4.07 us
    ppermute x1, starting transfers between devices, shards(): from_east = lax.ppermute(to_west, 'lat', [(b, a) for a, b in forward])  4.04 us
    pallas_call x1, Pallas kernels, shards(): pl.pallas_call(unpack_tracers, out_shape=jax.ShapeDtypeStruct(tracers.sha...  3.51 us
  transfers between devices with their start and end apart: 4, of which 2 were waited for; matrix products, arithmetic and copies ran while one was open for 0% of the time, Pallas kernels for 22%

commit v1 on v0

--- a/solution.py
+++ b/solution.py
@@ -4,6 +4,7 @@
 from jax.experimental import pallas as pl
 from jax.experimental.pallas import tpu as pltpu
 from jax.sharding import PartitionSpec as P
+
 
 STEPS = 2
 SUB = 2
@@ -123,7 +124,7 @@
         + side[..., :-2]
         - 4.0 * center
     )
-    chloro, top_light, absorbed = light_field(center[0])
+    chloro, top_light, _ = light_field(center[0])
     nutrient = center[1] * center[1]
     uptake = growth_rate * top_light * chloro * nutrient / (1.0 + nutrient)
     rate_cell = jnp.einsum("bst,bij->stij", rate_table, onehot, precision=lax.Precision.HIGHEST)
@@ -148,7 +149,7 @@
     ).astype(jnp.float32)
     state = ocean_state
     tracer_now = tracers
-    for cycle_index in range(STEPS):
+    for _ in range(STEPS):
         state = state * wet_mask[None]
         padded = extended(state, (("lat", 2),), 1, False)
         new_u, new_v, part_t, new_s, fluxes = ocean_core(padded, wet_mask, lat_start, total_lat)
@@ -157,7 +158,7 @@
         )
         tracer_now = tracer_now * sea_mask[None]
         flux_ext = extended(flux_t, (("lat", 2),), 1, True)
-        for sub_index in range(SUB):
+        for _ in range(SUB):
             tracer_ext = extended(tracer_now, (("lat", 2),), 1, True)
             tracer_now = tracer_core(tracer_ext, flux_ext, sea_mask, onehot, rate_table)
         heating = heat_gain * sea_mask * light_field(tracer_now[0])[2]
@@ -173,9 +174,10 @@
 LANES = 128
 TILE = 8
 FIELDS = 4
-
-
-def fits(ocean_state, tracers, rate_table, lat_count):
+GRANT = 16 * 1024 * 1024
+
+
+def fits(ocean_state, tracers, lat_count):
     _, levels, lat_rows, total_lon = ocean_state.shape
     species, _, columns, total_lat = tracers.shape
     return (
@@ -281,6 +283,32 @@
     east_ref[start : start + 2 * HALO, :] = spin(biome, HALO, 0)
 
 
+def fetch(sources, targets, ready):
+    copies = [pltpu.make_async_copy(a, b, ready.at[i]) for i, (a, b) in enumerate(zip(sources, targets, strict=True))]
+    for copy in copies:
+        copy.start()
+    return copies
+
+
+def pack(*refs):
+    sources, (packed_ref, west_ref, east_ref), (flat, depth) = refs[:5], refs[5:8], refs[8:10]
+    held, ready = refs[10:15], refs[15]
+    copies = fetch(sources, held, ready)
+    copies[0].wait()
+    copies[1].wait()
+    pack_ocean(held[0], held[1], packed_ref, flat, depth)
+    for copy in copies[2:]:
+        copy.wait()
+    pack_edges(held[2], held[3], held[4], west_ref, east_ref)
+
+
+def prepare_from(*refs):
+    sources, edges, outs, held, growth, ready = refs[:4], refs[4:6], refs[6:11], refs[11:15], refs[15], refs[16]
+    for copy in fetch(sources, held, ready):
+        copy.wait()
+    prepare(*held, *edges, *outs, growth)
+
+
 def light(plankton, surface):
     result = []
     depth = jnp.zeros(surface.shape, jnp.float32)
@@ -312,31 +340,48 @@
     return lit
 
 
-def spread_row(ref, index):
-    return ref[pl.ds(index, TILE, stride=0), :]
-
-
-def reaction(source_ref, base, rate_ref, growth_ref, row, levels, species):
-    sums = [[None, None] for _ in levels]
-    for kind in range(species):
-        rates = [
-            rate_ref[pl.ds((row * species + kind) * species + TILE * part, TILE), :] for part in range(2)
-        ]
-        for place, level in enumerate(levels):
-            value = spread_row(source_ref, base + (level * TILE + row) * species + kind)
-            for part in range(2):
-                term = rates[part] * value
-                sums[place][part] = term if sums[place][part] is None else sums[place][part] + term
-    index = rows_of()
+def rate_pieces(rate_table_ref):
+    kinds, species, _ = rate_table_ref.shape
+    rates = tracer_step * rate_table_ref[...].reshape(kinds * species, species)
+    high = rates.astype(jnp.bfloat16)
+    low = (rates - high.astype(jnp.float32)).astype(jnp.bfloat16)
+    return jnp.concatenate([high, low, high], axis=1)
+
+
+def reaction(source_ref, base, pieces, chosen, growth_ref, row, levels, species):
+    index = rows_of((species, LANES))
     sign = jnp.where(index == 0, 1.0, jnp.where(index == 1, -1.0, 0.0))
-    for place, level in enumerate(levels):
-        sums[place][0] = sums[place][0] + sign * spread_row(growth_ref, level * TILE + row)
+    sums = []
+    for pair in range(0, len(levels), 2):
+        near = levels[pair : pair + 2]
+        values = jnp.concatenate(
+            [source_ref[pl.ds(base + (level * TILE + row) * species, species), :] for level in near], axis=1
+        )
+        high = values.astype(jnp.bfloat16)
+        low = (values - high.astype(jnp.float32)).astype(jnp.bfloat16)
+        every = jnp.dot(
+            pieces, jnp.concatenate([high, high, low], axis=0), preferred_element_type=jnp.float32
+        )
+        for place, level in enumerate(near):
+            mine = every[:, place * LANES : (place + 1) * LANES]
+            total = mine[:species, :]
+            for kind, mask in enumerate(chosen):
+                total = jnp.where(mask, mine[(kind + 1) * species : (kind + 2) * species, :], total)
+            uptake = growth_ref[pl.ds(level * TILE + row, species, stride=0), :]
+            sums.append(total + sign * uptake)
     return sums
 
 
-def prepare(tracer_ref, sea_ref, biome_ref, rate_table_ref, from_west, from_east, now_ref, wet_ref, rate_ref, first_ref, growth, rate_columns):
+def biome_masks(biome_ref, row, kinds, species):
+    here = jnp.broadcast_to(biome_ref[row : row + 1, :], (species, LANES))
+    return [here == float(kind) for kind in range(1, kinds)]
+
+
+def prepare(
+    tracer_ref, sea_ref, biome_ref, rate_table_ref, from_west, from_east, now_ref, wet_ref, biomes_ref, pieces_ref,
+    first_ref, growth,
+):
     species, levels, columns, total_lat = tracer_ref.shape
-    kinds = rate_table_ref.shape[0]
     blocks = LANES // total_lat
     groups = levels // blocks
     own = columns // TILE
@@ -361,38 +406,30 @@
                 parts = [tracer_ref[kind, level, TILE * q : TILE * (q + 1), :] for q in range(own)]
                 whole = plane(parts, edge, block) * wet_ref[level * TILE : (level + 1) * TILE, :]
                 now_ref[pl.ds(level * TILE * species + kind, TILE, stride=species), :] = whole
-    start = (species + 1) * groups * HALO
     parts = [biome_ref[TILE * q : TILE * (q + 1), :].astype(jnp.float32) for q in range(own)]
-    biome = plane(parts, halo(start), 0)
-    for b in range(kinds):
-        for kind in range(species):
-            for part in range(2):
-                column = rate_table_ref[b, TILE * part : TILE * (part + 1), kind : kind + 1]
-                rate_columns[pl.ds(((b * species + kind) * 2 + part) * TILE, TILE), :] = tracer_step * jnp.broadcast_to(column, (TILE, LANES))
-    for row in range(TILE):
-        here = jnp.broadcast_to(biome[row : row + 1, :], (TILE, LANES))
-        chosen = [here == float(b) for b in range(kinds)]
-        for kind in range(species):
-            for part in range(2):
-                rate = jnp.zeros((TILE, LANES), jnp.float32)
-                for b in range(kinds):
-                    rate = jnp.where(chosen[b], rate_columns[pl.ds(((b * species + kind) * 2 + part) * TILE, TILE), :], rate)
-                rate_ref[pl.ds((row * species + kind) * species + TILE * part, TILE), :] = rate
+    biomes_ref[...] = plane(parts, halo((species + 1) * groups * HALO), 0)
+    pieces = rate_pieces(rate_table_ref)
+    pieces_ref[...] = pieces
     put_growth(growth, now_ref, levels, species, total_lat)
 
     def react(group, carry):
         near = [group * 4 + i for i in range(4)]
         for row in range(TILE):
-            for level, sums in zip(near, reaction(now_ref, 0, rate_ref, growth, row, near, species), strict=True):
-                for part in range(2):
-                    first_ref[pl.ds((level * TILE + row) * species + TILE * part, TILE), :] = sums[part]
+            chosen = biome_masks(biomes_ref, row, rate_table_ref.shape[0], species)
+            sums = reaction(now_ref, 0, pieces, chosen, growth, row, near, species)
+            for level, change in zip(near, sums, strict=True):
+                first_ref[pl.ds((level * TILE + row) * species, species), :] = change
         return carry
 
     lax.fori_loop(0, levels // 4, react, 0)
 
 
-def advance(received, now_ref, wet_ref, rate_ref, first_ref, sent, last_ref, work, ocean, coef, tracer, growth, sizes):
-    levels, species, total_lat, columns = sizes
+def advance(
+    received, now_ref, wet_ref, biomes_ref, pieces_ref, first_ref, sent_out, last_out, sent, last_ref, work, ocean, coef,
+    tracer, growth, done, sizes,
+):
+    levels, species, total_lat, columns, kinds = sizes
+    pieces = pieces_ref[...]
     count = total_lat // 2
     own = columns // TILE
     half = FIELDS * levels
@@ -462,18 +499,22 @@
             new_v.append(wet[k] * (v + time_step * (-spin_rate * u - slope_north + viscosity * lap_v)))
             spread.append(0.5 * (u_east - u_west) + 0.5 * (v_north - v_south))
             face_east = 0.5 * (u + u_east)
+            face_west = west(face_east)
             face_north = jnp.where(lat == total_lat - 1, 0.0, 0.5 * (v + v_north))
+            face_south = spin(face_north, 1, 1)
             up_east, down_east = jnp.maximum(face_east, 0.0), jnp.minimum(face_east, 0.0)
+            up_west, down_west = jnp.maximum(face_west, 0.0), jnp.minimum(face_west, 0.0)
             up_north, down_north = jnp.maximum(face_north, 0.0), jnp.minimum(face_north, 0.0)
+            up_south, down_south = jnp.maximum(face_south, 0.0), jnp.minimum(face_south, 0.0)
             mask = tracer_step * sea[k]
             at = step * 7 * plane + k * TILE
             coef[pl.ds(at + plane, TILE), :] = mask * (tracer_diff - down_east)
-            coef[pl.ds(at + 2 * plane, TILE), :] = mask * (tracer_diff + west(up_east))
+            coef[pl.ds(at + 2 * plane, TILE), :] = mask * (tracer_diff + up_west)
             coef[pl.ds(at + 3 * plane, TILE), :] = jnp.where(
                 lat == total_lat - 1, 0.0, mask * (tracer_diff - down_north)
             )
-            coef[pl.ds(at + 4 * plane, TILE), :] = jnp.where(lat == 0, 0.0, mask * (tracer_diff + south(up_north)))
-            coef[pl.ds(at, TILE), :] = -4.0 * tracer_diff - up_east + west(down_east) - up_north + south(down_north)
+            coef[pl.ds(at + 4 * plane, TILE), :] = jnp.where(lat == 0, 0.0, mask * (tracer_diff + up_south))
+            coef[pl.ds(at, TILE), :] = -4.0 * tracer_diff - up_east + down_west - up_north + down_south
         total = jnp.zeros((TILE, LANES), jnp.float32)
         below_up, below_down = total, total
         for k in reversed(range(levels)):
@@ -504,32 +545,29 @@
             near = [group * 4 + i for i in range(4)]
             for r in range(TILE):
                 if ready is None:
-                    sums = reaction(source, base, rate_ref, growth, r, near, species)
+                    chosen = biome_masks(biomes_ref, r, kinds, species)
+                    sums = reaction(source, base, pieces, chosen, growth, r, near, species)
                 for place, level in enumerate(near):
                     cell = level * TILE + r
-                    weight = [spread_row(coef, start + i * plane + cell) for i in range(7)]
-                    mask = spread_row(wet_ref, cell)
                     above = jnp.maximum(level - 1, 0) * TILE + r
                     under = jnp.minimum(level + 1, levels - 1) * TILE + r
-                    for part in range(2):
-
-                        def take(index, part=part):
-                            return source[pl.ds(base + index * species + TILE * part, TILE), :]
-
-                        x = take(cell)
-                        x_east = take(cell + 1) if r < TILE - 1 else spin(take(cell - r), -total_lat, 1)
-                        x_west = take(cell - 1) if r > 0 else spin(take(cell + TILE - 1), total_lat, 1)
-                        if ready is None:
-                            change = sums[place][part]
-                        else:
-                            change = ready[pl.ds(cell * species + TILE * part, TILE), :]
-                        value = (
-                            (weight[0] * x + weight[1] * x_east)
-                            + (weight[2] * x_west + weight[3] * spin(x, -1, 1))
-                            + (weight[4] * spin(x, 1, 1) + weight[5] * take(above))
-                            + (weight[6] * take(under) + mask * change)
-                        )
-                        target[pl.ds(target_base + cell * species + TILE * part, TILE), :] = value
+                    weight = [coef[pl.ds(start + i * plane + cell, species, stride=0), :] for i in range(7)]
+                    mask = wet_ref[pl.ds(cell, species, stride=0), :]
+
+                    def take(index):
+                        return source[pl.ds(base + index * species, species), :]
+
+                    x = take(cell)
+                    x_east = take(cell + 1) if r < TILE - 1 else spin(take(cell - r), -total_lat, 1)
+                    x_west = take(cell - 1) if r > 0 else spin(take(cell + TILE - 1), total_lat, 1)
+                    change = sums[place] if ready is None else ready[pl.ds(cell * species, species), :]
+                    value = (
+                        (weight[0] * x + weight[1] * x_east)
+                        + (weight[2] * x_west + weight[3] * spin(x, -1, 1))
+                        + (weight[4] * spin(x, 1, 1) + weight[5] * take(above))
+                        + (weight[6] * take(under) + mask * change)
+                    )
+                    target[pl.ds(target_base + cell * species, species), :] = value
             return carry
 
         lax.fori_loop(0, levels // 4, body, 0)
@@ -549,6 +587,9 @@
                 put_growth(growth, source, levels, species, total_lat, base)
             substep(step, source, base, target, target_base, first_ref if first else None)
             source, base = target, target_base
+        if step == STEPS - 1:
+            keep = pltpu.make_async_copy(last_ref, last_out, done.at[0])
+            keep.start()
         lit = light(planes_of(source, 0, levels, species, base), surface_light(total_lat))
         warm = []
         for k, x in enumerate(read(2)):
@@ -567,6 +608,10 @@
                 sent[pl.ds(q * TILE + j * 4 + r_low, count, stride=own * TILE), :] = work[
                     pl.ds(r_low * LANES + q * total_lat + j, count, stride=2), :
                 ]
+    send = pltpu.make_async_copy(sent, sent_out, done.at[1])
+    send.start()
+    send.wait()
+    keep.wait()
 
 
 def unpack_tracers(last_ref, out_ref):
@@ -594,13 +639,21 @@
     return [pltpu.VMEM(shape, jnp.float32) for shape in shapes]
 
 
-def real(*shape):
-    return jax.ShapeDtypeStruct(shape, jnp.float32)
+def far(*shape):
+    return pltpu.HBM(shape, jnp.float32)
+
+
+def near(*shape, dtype=jnp.float32):
+    return pltpu.VMEM(shape, dtype)
+
+
+def placed(space, *arrays):
+    return [pltpu.with_memory_space_constraint(x, space) for x in arrays]
 
 
 def shards(ocean_state, bottom, tracers, land_sea, biome_id, rate_table):
     count = lax.axis_size("lat")
-    if not fits(ocean_state, tracers, rate_table, count):
+    if not fits(ocean_state, tracers, count):
         return general_shards(ocean_state, bottom, tracers, land_sea, biome_id, rate_table)
     _, levels, _, total_lon = ocean_state.shape
     species, _, columns, total_lat = tracers.shape
@@ -608,56 +661,89 @@
     size = cells * species
     own = columns // TILE
 
-    packed = pl.pallas_call(
-        pack_ocean,
-        out_shape=real(count * (own + 1) * TILE, LANES),
-        scratch_shapes=grids((LANES, total_lon), (TILE, total_lon)),
-        name="pack_ocean",
-    )(ocean_state, bottom)
+    edge_rows = (species + 1) * (levels * total_lat // LANES) * HALO + 2 * HALO
+    forward = [(i, (i + 1) % count) for i in range(count)]
+    backward = [(b, a) for a, b in forward]
+    kinds = rate_table.shape[0]
+    roomy = pltpu.CompilerParams(vmem_limit_bytes=GRANT)
+    ocean_state, bottom, tracers, land_sea, biome_id, rate_table = placed(
+        pltpu.HBM, ocean_state, bottom, tracers, land_sea, biome_id, rate_table
+    )
+    vmem = pl.BlockSpec(memory_space=pltpu.VMEM)
+    hbm = pl.BlockSpec(memory_space=pltpu.HBM)
+
+    packed, to_west, to_east = pl.pallas_call(
+        pack,
+        out_shape=[far(count * (own + 1) * TILE, LANES), far(edge_rows, LANES), far(edge_rows, LANES)],
+        in_specs=[hbm] * 5,
+        out_specs=[vmem] * 3,
+        scratch_shapes=grids((LANES, total_lon), (TILE, total_lon))
+        + [pltpu.VMEM(x.shape, x.dtype) for x in (ocean_state, bottom, tracers, land_sea, biome_id)]
+        + [pltpu.SemaphoreType.DMA((5,))],
+        compiler_params=roomy,
+        name="pack",
+    )(ocean_state, bottom, tracers, land_sea, biome_id)
+    from_west = lax.ppermute(to_east, "lat", forward)
+    from_east = lax.ppermute(to_west, "lat", backward)
     received = lax.all_to_all(
         packed.reshape(count, (own + 1) * TILE, LANES), "lat", split_axis=0, concat_axis=0, tiled=True
     ).reshape(packed.shape)
-
-    edge_rows = (species + 1) * (levels * total_lat // LANES) * HALO + 2 * HALO
-    to_west, to_east = pl.pallas_call(
-        pack_edges, out_shape=[real(edge_rows, LANES)] * 2, name="pack_edges"
-    )(tracers, land_sea, biome_id)
-    forward = [(i, (i + 1) % count) for i in range(count)]
-    from_west = lax.ppermute(to_east, "lat", forward)
-    from_east = lax.ppermute(to_west, "lat", [(b, a) for a, b in forward])
-
-    now, wet, rates, first = pl.pallas_call(
-        prepare,
-        out_shape=[real(size, LANES), real(cells, LANES), real(TILE * species * species, LANES), real(size, LANES)],
-        scratch_shapes=grids((cells, LANES), (rate_table.shape[0] * species * 2 * TILE, LANES)),
+    from_west, from_east, received = placed(pltpu.VMEM, from_west, from_east, received)
+
+    now, wet, biomes, pieces, first = pl.pallas_call(
+        prepare_from,
+        out_shape=[
+            near(size, LANES),
+            near(cells, LANES),
+            near(TILE, LANES),
+            near(kinds * species, 3 * species, dtype=jnp.bfloat16),
+            near(size, LANES),
+        ],
+        in_specs=[hbm] * 4 + [vmem] * 2,
+        out_specs=[vmem] * 5,
+        scratch_shapes=[pltpu.VMEM(x.shape, x.dtype) for x in (tracers, land_sea, biome_id, rate_table)]
+        + grids((cells, LANES))
+        + [pltpu.SemaphoreType.DMA((4,))],
+        compiler_params=roomy,
         name="prepare",
     )(tracers, land_sea, biome_id, rate_table, from_west, from_east)
 
     def run(*refs):
-        advance(*refs, (levels, species, total_lat, columns))
+        advance(*refs, (levels, species, total_lat, columns, kinds))
 
     sent, last = pl.pallas_call(
         run,
-        out_shape=[real(count * own * TILE, LANES), real(size, LANES)],
+        out_shape=[far(count * own * TILE, LANES), far(size, LANES)],
+        in_specs=[vmem] * 6,
+        out_specs=[hbm] * 2,
         scratch_shapes=grids(
+            (count * own * TILE, LANES),
+            (size, LANES),
             (4 * LANES, LANES),
             (FIELDS * cells, LANES),
             (STEPS * 7 * cells, LANES),
             (2 * size, LANES),
             (cells, LANES),
-        ),
+        )
+        + [pltpu.SemaphoreType.DMA((2,))],
+        compiler_params=roomy,
         name="advance",
-    )(received, now, wet, rates, first)
+    )(received, now, wet, biomes, pieces, first)
     back = lax.all_to_all(
         sent.reshape(count, own * TILE, LANES), "lat", split_axis=0, concat_axis=0, tiled=True
     ).reshape(sent.shape)
+    (back,) = placed(pltpu.VMEM, back)
+    (last,) = placed(pltpu.HBM, last)
     tracers_out = pl.pallas_call(
-        unpack_tracers, out_shape=jax.ShapeDtypeStruct(tracers.shape, jnp.float32), name="unpack_tracers"
+        unpack_tracers, out_shape=far(*tracers.shape), name="unpack_tracers"
     )(last)
     state_out = pl.pallas_call(
         unpack_ocean,
-        out_shape=jax.ShapeDtypeStruct(ocean_state.shape, jnp.float32),
+        out_shape=far(*ocean_state.shape),
+        in_specs=[vmem],
+        out_specs=vmem,
         scratch_shapes=grids((total_lon, LANES), (LANES, total_lon)),
+        compiler_params=roomy,
         name="unpack_ocean",
     )(back)
     return (state_out, tracers_out)

time: 58.4 us -> 49.6 us (0.85)
  Pallas kernels: 29.2 us -> 20.6 us
  waiting for transfers between devices: 9.56 us -> 12.5 us
  local copies, waits for them, and re-layouts: 2.69 us -> 0 us
    pallas_call x6 -> x5, Pallas kernels: 29.2 us -> 20.6 us  [the longest x1 9.13 us: shards(): pl.pallas_call(run, out_shape=[far(count * own * TILE, LANES), far(size,...]
    ppermute x1, waiting for transfers between devices: 4.1 us -> 7.05 us  [shards(): from_west = lax.ppermute(to_east, 'lat', forward)]
    unnamed x8 -> x0, local copies, waits for them, and re-layouts: 2.69 us -> none
  transfers between devices with their start and end apart: 4 -> 4, of which waited for: 2 -> 2; matrix products, arithmetic and copies ran while one was open for 0% -> 0% of each run, Pallas kernels for 22% -> 15%
where the time goes in v1:
time: 49.6 us; the launch traced here: 49.2 us
  Pallas kernels  20.6 us (42%)
  starting transfers between devices  15.5 us (31%)
  waiting for transfers between devices  12.5 us (25%)
  between operations  0.68 us (1%)
    pallas_call x1, Pallas kernels, shards(): pl.pallas_call(run, out_shape=[far(count * own * TILE, LANES), far(size,...  9.13 us
    all_to_all x1, starting transfers between devices, shards(): lax.all_to_all(packed.reshape(count, (own + 1) * TILE, LANES), 'lat', spl...  7.43 us
    ppermute x1, waiting for transfers between devices, shards(): from_west = lax.ppermute(to_east, 'lat', forward)  7.05 us
    all_to_all x1, waiting for transfers between devices, shards(): lax.all_to_all(sent.reshape(count, own * TILE, LANES), 'lat', split_axis=...  5.42 us
    ppermute x1, starting transfers between devices, shards(): from_east = lax.ppermute(to_west, 'lat', backward)  4.08 us
    pallas_call x1, Pallas kernels, shards(): pl.pallas_call(prepare_from, out_shape=[near(size, LANES), near(cells, LA...  4 us
    all_to_all x1, starting transfers between devices, shards(): lax.all_to_all(sent.reshape(count, own * TILE, LANES), 'lat', split_axis=...  3.53 us
    pallas_call x1, Pallas kernels, shards(): pl.pallas_call(unpack_tracers, out_shape=far(*tracers.shape), name='unpac...  3.51 us
  transfers between devices with their start and end apart: 4, of which 2 were waited for; matrix products, arithmetic and copies ran while one was open for 0% of the time, Pallas kernels for 15%

profile of v1, /device:TPU:0, one launch (start us, length us, event | category | flops | bytes accessed | tf_op | source)
XLA Modules:
  0.0 49.2 jit_solution(5181580078543670814)
XLA Ops:
  0.6 3.1 %pack.1 = (f32[512,128]{1,0:T(8,128)}, f32[280,128]{1,0:T(8,128)}, f32[280,128]{1,0:T(8,128)}) custom-call(f32[4,16,2,384]{3,2,1,0:T(2,128)} %refs_0_.2, s32[2,384]{1,0:T(2,128)} %refs_1_.2, f32[16,16,24,32]{3,2,1,0:T(8,128)} %refs_0_.3, s32[16,24,32]{2,1,0:T(8,128)} %refs_1_.3, s32[24,32]{1,0:T(8,128)} %refs_2_.3), custom_call_target="tpu_custom_call" | custom-call | tf_op jit(solution)/shard_map/pack/pallas_call | solution.py:675
  3.7 7.4 %all-to-all-start = ((f32[16,32,128]{2,1,0:T(8,128)}), f32[16,32,128]{2,1,0:T(8,128)S(1)}, u32[]{:S(2)}, u32[]{:S(2)}) async-start(f32[16,32,128]{2,1,0:T(8,128)} %bitcast.6), calls=%async_computation | async-start | bytes 524288 | tf_op jit(solution)/shard_map/all_to_all | solution.py:688
  11.1 0.4 collective-permute-start
  11.5 4.1 %collective-permute-start.1 = (f32[280,128]{1,0:T(8,128)}, f32[280,128]{1,0:T(8,128)S(1)}, u32[]{:S(2)}, u32[]{:S(2)}) collective-permute-start(f32[280,128]{1,0:T(8,128)} %get-tuple-element.14), channel_id=1, source_target_pairs={{1,0},{2,1},{3,2},{4,3},{5,4},{6,5},{7,6},{8,7},{9,8},{10,9},{11,1... | collective-permute-start | bytes 430088 | tf_op jit(solution)/shard_map/ppermute | solution.py:687
  15.6 7.1 %collective-permute-done.refs_4_ = f32[280,128]{1,0:T(8,128)S(1)} collective-permute-done((f32[280,128]{1,0:T(8,128)}, f32[280,128]{1,0:T(8,128)S(1)}, u32[]{:S(2)}, u32[]{:S(2)}) %collective-permute-start) | collective-permute-done | bytes 143392 | tf_op jit(solution)/shard_map/ppermute | solution.py:686
  22.7 0.0 collective-permute-done.1.refs_5_
  22.7 4.0 %prepare.1 = (f32[2048,128]{1,0:T(8,128)S(1)}, f32[128,128]{1,0:T(8,128)S(1)}, f32[8,128]{1,0:T(8,128)S(1)}, bf16[64,48]{1,0:T(8,128)(2,1)S(1)}, f32[2048,128]{1,0:T(8,128)S(1)}) custom-call(f32[16,16,24,32]{3,2,1,0:T(8,128)} %refs_0_.3, s32[16,24,32]{2,1,0:T(8,128)} %refs_1_.3, s32[24,32]{1,0:T(8,128)} %refs_2_.3, f32[4,16,16]{2,1,0:T(8,128)} %refs_3_.3, ...), custom_call_target="tpu_custom_call" | custom-call | tf_op jit(solution)/shard_map/prepare/pallas_call | solution.py:693
  26.7 0.0 all-to-all-done
  26.7 9.1 %advance.1 = (f32[384,128]{1,0:T(8,128)}, f32[2048,128]{1,0:T(8,128)}) custom-call(f32[512,128]{1,0:T(8,128)S(1)} %bitcast.4, f32[2048,128]{1,0:T(8,128)S(1)} %get-tuple-element.15.refs_1_, f32[128,128]{1,0:T(8,128)S(1)} %get-tuple-element.16.refs_2_, f32[8,128]{1,0:T(8,128)S(1)} %get-tuple-element.17.refs_3_, bf16[64,48]{1,0:T(8,128)(2,1)S(1)} %get-tuple-element.18.refs_4_, ...), custom_call_target="tpu_custom_call" | custom-call | tf_op jit(solution)/shard_map/advance/pallas_call | solution.py:714
  35.8 3.5 %all-to-all-start.1 = ((f32[16,24,128]{2,1,0:T(8,128)}), f32[16,24,128]{2,1,0:T(8,128)S(1)}, u32[]{:S(2)}, u32[]{:S(2)}) async-start(f32[16,24,128]{2,1,0:T(8,128)} %bitcast.7), calls=%async_computation.1 | async-start | bytes 393216 | tf_op jit(solution)/shard_map/all_to_all | solution.py:732
  39.4 3.5 %unpack_tracers.1 = f32[16,16,24,32]{3,2,1,0:T(8,128)} custom-call(f32[2048,128]{1,0:T(8,128)} %get-tuple-element.21.last_ref), custom_call_target="tpu_custom_call" | custom-call | tf_op jit(solution)/shard_map/unpack_tracers/pallas_call | solution.py:737
  42.9 5.4 %all-to-all-done.1 = f32[16,24,128]{2,1,0:T(8,128)S(1)} async-done(((f32[16,24,128]{2,1,0:T(8,128)}), f32[16,24,128]{2,1,0:T(8,128)S(1)}, u32[]{:S(2)}, u32[]{:S(2)}) %all-to-all-start.1) | async-done | bytes 196640 | tf_op jit(solution)/shard_map/all_to_all | solution.py:732
  48.3 0.9 %unpack_ocean.1 = f32[4,16,2,384]{3,2,1,0:T(2,128)} custom-call(f32[384,128]{1,0:T(8,128)S(1)} %bitcast.5), custom_call_target="tpu_custom_call" | custom-call | tf_op jit(solution)/shard_map/unpack_ocean/pallas_call | solution.py:740
Async XLA Ops:
  3.7 23.0 %all-to-all-start = ((f32[16,32,128]{2,1,0:T(8,128)}), f32[16,32,128]{2,1,0:T(8,128)S(1)}, u32[]{:S(2)}, u32[]{:S(2)}) async-start(f32[16,32,128]{2,1,0:T(8,128)} %bitcast.6), calls=%async_computation | async-start | bytes 524288 | tf_op jit(solution)/shard_map/all_to_all | solution.py:688
  11.1 11.5 %collective-permute-start = (f32[280,128]{1,0:T(8,128)}, f32[280,128]{1,0:T(8,128)S(1)}, u32[]{:S(2)}, u32[]{:S(2)}) collective-permute-start(f32[280,128]{1,0:T(8,128)} %get-tuple-element.13), channel_id=1, source_target_pairs={{0,1},{1,2},{2,3},{3,4},{4,5},{5,6},{6,7},{7,8},{8,9},{9,10},{10,1... | collective-permute-start | bytes 430088 | tf_op jit(solution)/shard_map/ppermute | solution.py:686
  11.5 11.1 %collective-permute-start.1 = (f32[280,128]{1,0:T(8,128)}, f32[280,128]{1,0:T(8,128)S(1)}, u32[]{:S(2)}, u32[]{:S(2)}) collective-permute-start(f32[280,128]{1,0:T(8,128)} %get-tuple-element.14), channel_id=1, source_target_pairs={{1,0},{2,1},{3,2},{4,3},{5,4},{6,5},{7,6},{8,7},{9,8},{10,9},{11,1... | collective-permute-start | bytes 430088 | tf_op jit(solution)/shard_map/ppermute | solution.py:687
  35.8 12.5 %all-to-all-start.1 = ((f32[16,24,128]{2,1,0:T(8,128)}), f32[16,24,128]{2,1,0:T(8,128)S(1)}, u32[]{:S(2)}, u32[]{:S(2)}) async-start(f32[16,24,128]{2,1,0:T(8,128)} %bitcast.7), calls=%async_computation.1 | async-start | bytes 393216 | tf_op jit(solution)/shard_map/all_to_all | solution.py:732

commit v2 on v1

--- a/solution.py
+++ b/solution.py
@@ -192,6 +192,7 @@
         and levels <= columns + HALO
         and 2 * columns + 3 * HALO <= FIELDS * levels
         and species == 2 * TILE
+        and lat_count % 2 == 0
         and levels % (LANES // total_lat) == 0
     )
 
@@ -246,12 +247,20 @@
         out_ref[pl.ds((target * (own + 1) + own) * TILE, TILE), :] = jnp.where(window, level_line, edge)
 
 
-def pack_edges(tracer_ref, sea_ref, biome_ref, west_ref, east_ref):
-    species, levels, columns, total_lat = tracer_ref.shape
+def pack_edges(low_ref, high_ref, sea_ref, biome_ref, first_ref, second_ref, even):
+    species, levels, _, total_lat = low_ref.shape
+    columns = sea_ref.shape[1]
     blocks = LANES // total_lat
     groups = levels // blocks
     low = rows_of((TILE, total_lat)) < HALO
     last = columns - TILE
+
+    def put(start, both):
+        flipped = spin(both, HALO, 0)
+        here = jnp.where(even, flipped, both)
+        first_ref[start : start + HALO, :] = here[:HALO, :]
+        second_ref[start : start + HALO, :] = here[HALO:, :]
+
     for group in range(groups):
         wet = [
             jnp.where(low, sea_ref[group * blocks + b, 0:TILE, :], sea_ref[group * blocks + b, last:columns, :]).astype(
@@ -260,27 +269,18 @@
             for b in range(blocks)
         ]
         joined = jnp.concatenate(wet, axis=1)
-        start = species * groups * HALO + group * HALO
-        west_ref[start : start + HALO, :] = joined[:HALO, :]
-        east_ref[start : start + HALO, :] = joined[HALO:, :]
+        put(species * groups * HALO + group * HALO, joined)
         for kind in range(species):
             parts = [
-                jnp.where(
-                    low,
-                    tracer_ref[kind, group * blocks + b, 0:TILE, :],
-                    tracer_ref[kind, group * blocks + b, last:columns, :],
-                )
+                jnp.where(low, low_ref[kind, group * blocks + b], high_ref[kind, group * blocks + b])
                 for b in range(blocks)
             ]
-            both = jnp.concatenate(parts, axis=1) * joined
-            start = (kind * groups + group) * HALO
-            west_ref[start : start + HALO, :] = both[:HALO, :]
-            east_ref[start : start + HALO, :] = both[HALO:, :]
+            put((kind * groups + group) * HALO, jnp.concatenate(parts, axis=1) * joined)
     biome = jnp.where(low, biome_ref[0:TILE, :], biome_ref[last:columns, :]).astype(jnp.float32)
-    biome = jnp.concatenate([biome] * blocks, axis=1)
     start = (species + 1) * groups * HALO
-    west_ref[start : start + 2 * HALO, :] = biome
-    east_ref[start : start + 2 * HALO, :] = spin(biome, HALO, 0)
+    put(start, jnp.concatenate([biome] * blocks, axis=1))
+    first_ref[start + HALO : start + 2 * HALO, :] = jnp.zeros((HALO, LANES), jnp.float32)
+    second_ref[start + HALO : start + 2 * HALO, :] = jnp.zeros((HALO, LANES), jnp.float32)
 
 
 def fetch(sources, targets, ready):
@@ -290,30 +290,31 @@
     return copies
 
 
-def pack(*refs):
-    sources, (packed_ref, west_ref, east_ref), (flat, depth) = refs[:5], refs[5:8], refs[8:10]
-    held, ready = refs[10:15], refs[15]
+def is_even():
+    return lax.axis_index("lat") % 2 == 0
+
+
+def pack(ocean, bottom, tracers, sea, biome, *refs):
+    out, edges, (flat, depth), held, result, ready, gone = refs[0], refs[1:3], refs[3:5], refs[5:11], refs[11], refs[12], refs[13]
+    columns = tracers.shape[2]
+    sources = [ocean, bottom, tracers.at[:, :, 0:TILE, :], tracers.at[:, :, columns - TILE : columns, :], sea, biome]
     copies = fetch(sources, held, ready)
     copies[0].wait()
     copies[1].wait()
-    pack_ocean(held[0], held[1], packed_ref, flat, depth)
+    pack_ocean(held[0], held[1], result, flat, depth)
+    leaving = pltpu.make_async_copy(result, out, gone)
+    leaving.start()
     for copy in copies[2:]:
         copy.wait()
-    pack_edges(held[2], held[3], held[4], west_ref, east_ref)
-
-
-def prepare_from(*refs):
-    sources, edges, outs, held, growth, ready = refs[:4], refs[4:6], refs[6:11], refs[11:15], refs[15], refs[16]
-    for copy in fetch(sources, held, ready):
-        copy.wait()
-    prepare(*held, *edges, *outs, growth)
+    pack_edges(*held[2:], *edges, is_even())
+    leaving.wait()
 
 
 def light(plankton, surface):
     result = []
     depth = jnp.zeros(surface.shape, jnp.float32)
     for value in plankton:
-        chloro = jnp.maximum(value, 0.0) + jnp.log1p(jnp.exp(-jnp.abs(value)))
+        chloro = jnp.maximum(value, 0.0) + jnp.log(1.0 + jnp.exp(-jnp.abs(value)))
         attenuate = water_atten + chl_atten * chloro
         result.append((chloro, surface * jnp.exp(-depth), attenuate))
         depth = depth + attenuate
@@ -349,7 +350,7 @@
 
 
 def reaction(source_ref, base, pieces, chosen, growth_ref, row, levels, species):
-    index = rows_of((species, LANES))
+    index = rows_of()
     sign = jnp.where(index == 0, 1.0, jnp.where(index == 1, -1.0, 0.0))
     sums = []
     for pair in range(0, len(levels), 2):
@@ -367,8 +368,8 @@
             total = mine[:species, :]
             for kind, mask in enumerate(chosen):
                 total = jnp.where(mask, mine[(kind + 1) * species : (kind + 2) * species, :], total)
-            uptake = growth_ref[pl.ds(level * TILE + row, species, stride=0), :]
-            sums.append(total + sign * uptake)
+            uptake = sign * growth_ref[pl.ds(level * TILE + row, TILE, stride=0), :]
+            sums.append(jnp.concatenate([total[:TILE, :] + uptake, total[TILE:, :]], axis=0))
     return sums
 
 
@@ -377,51 +378,67 @@
     return [here == float(kind) for kind in range(1, kinds)]
 
 
-def prepare(
-    tracer_ref, sea_ref, biome_ref, rate_table_ref, from_west, from_east, now_ref, wet_ref, biomes_ref, pieces_ref,
-    first_ref, growth,
+def prepare_own(tracers, sea, biome, rate_table, own_ref, wet_ref, biomes_ref, pieces_ref, *refs):
+    held, ready = refs[:4], refs[4]
+    tracer_ref, sea_ref, biome_ref, rate_table_ref = held
+    species, levels, columns, total_lat = tracers.shape
+    own = columns // TILE
+    copies = fetch([tracers, sea, biome, rate_table], held, ready)
+    blank = jnp.zeros((TILE, total_lat), jnp.float32)
+    for copy in copies[1:]:
+        copy.wait()
+
+    def plane(parts):
+        return jnp.concatenate(parts + [blank], axis=1)
+
+    pieces_ref[...] = rate_pieces(rate_table_ref)
+    biomes_ref[...] = plane([biome_ref[TILE * q : TILE * (q + 1), :].astype(jnp.float32) for q in range(own)])
+    for level in range(levels):
+        parts = [sea_ref[level, TILE * q : TILE * (q + 1), :].astype(jnp.float32) for q in range(own)]
+        wet_ref[level * TILE : (level + 1) * TILE, :] = plane(parts)
+    copies[0].wait()
+    for level in range(levels):
+        wet = wet_ref[level * TILE : (level + 1) * TILE, :]
+        for kind in range(species):
+            parts = [tracer_ref[kind, level, TILE * q : TILE * (q + 1), :] for q in range(own)]
+            own_ref[pl.ds(level * TILE * species + kind, TILE, stride=species), :] = plane(parts) * wet
+
+
+def prepare_all(
+    own_ref, own_wet_ref, own_biomes_ref, pieces_ref, from_first, from_second, now_ref, wet_ref, biomes_ref, first_ref, growth, sizes
 ):
-    species, levels, columns, total_lat = tracer_ref.shape
+    levels, species, total_lat, columns, kinds = sizes
     blocks = LANES // total_lat
     groups = levels // blocks
-    own = columns // TILE
+    inner = lanes_of() < columns // TILE * total_lat
+    even = is_even()
 
     def halo(start):
-        return jnp.concatenate([from_east[start : start + HALO, :], from_west[start : start + HALO, :]], axis=0)
-
-    def plane(parts, edge, block):
-        return jnp.concatenate(parts + [edge[:, block * total_lat : (block + 1) * total_lat]], axis=1)
+        both = jnp.concatenate([from_first[start : start + HALO, :], from_second[start : start + HALO, :]], axis=0)
+        return jnp.where(even, both, spin(both, HALO, 0))
+
+    def joined(inside, edge, block):
+        return jnp.where(inner, inside, spin(edge, LANES - (block + 1) * total_lat, 1))
 
     for group in range(groups):
         edge = halo((species * groups + group) * HALO)
         for block in range(blocks):
-            level = group * blocks + block
-            parts = [sea_ref[level, TILE * q : TILE * (q + 1), :].astype(jnp.float32) for q in range(own)]
-            wet_ref[level * TILE : (level + 1) * TILE, :] = plane(parts, edge, block)
+            place = slice((group * blocks + block) * TILE, (group * blocks + block + 1) * TILE)
+            wet_ref[place, :] = joined(own_wet_ref[place, :], edge, block)
+    biomes_ref[...] = joined(own_biomes_ref[...], halo((species + 1) * groups * HALO), 0)
     for kind in range(species):
         for group in range(groups):
             edge = halo((kind * groups + group) * HALO)
             for block in range(blocks):
-                level = group * blocks + block
-                parts = [tracer_ref[kind, level, TILE * q : TILE * (q + 1), :] for q in range(own)]
-                whole = plane(parts, edge, block) * wet_ref[level * TILE : (level + 1) * TILE, :]
-                now_ref[pl.ds(level * TILE * species + kind, TILE, stride=species), :] = whole
-    parts = [biome_ref[TILE * q : TILE * (q + 1), :].astype(jnp.float32) for q in range(own)]
-    biomes_ref[...] = plane(parts, halo((species + 1) * groups * HALO), 0)
-    pieces = rate_pieces(rate_table_ref)
-    pieces_ref[...] = pieces
+                place = pl.ds((group * blocks + block) * TILE * species + kind, TILE, stride=species)
+                now_ref[place, :] = joined(own_ref[place, :], edge, block)
     put_growth(growth, now_ref, levels, species, total_lat)
-
-    def react(group, carry):
-        near = [group * 4 + i for i in range(4)]
-        for row in range(TILE):
-            chosen = biome_masks(biomes_ref, row, rate_table_ref.shape[0], species)
-            sums = reaction(now_ref, 0, pieces, chosen, growth, row, near, species)
-            for level, change in zip(near, sums, strict=True):
-                first_ref[pl.ds((level * TILE + row) * species, species), :] = change
-        return carry
-
-    lax.fori_loop(0, levels // 4, react, 0)
+    pieces = pieces_ref[...]
+    for row in range(TILE):
+        chosen = biome_masks(biomes_ref, row, kinds, species)
+        every = list(range(levels))
+        for level, change in zip(every, reaction(now_ref, 0, pieces, chosen, growth, row, every, species), strict=True):
+            first_ref[pl.ds((level * TILE + row) * species, species), :] = change
 
 
 def advance(
@@ -549,8 +566,8 @@
                     sums = reaction(source, base, pieces, chosen, growth, r, near, species)
                 for place, level in enumerate(near):
                     cell = level * TILE + r
-                    above = jnp.maximum(level - 1, 0) * TILE + r
-                    under = jnp.minimum(level + 1, levels - 1) * TILE + r
+                    above = max(level - 1, 0) * TILE + r
+                    under = min(level + 1, levels - 1) * TILE + r
                     weight = [coef[pl.ds(start + i * plane + cell, species, stride=0), :] for i in range(7)]
                     mask = wet_ref[pl.ds(cell, species, stride=0), :]
 
@@ -570,7 +587,8 @@
                     target[pl.ds(target_base + cell * species, species), :] = value
             return carry
 
-        lax.fori_loop(0, levels // 4, body, 0)
+        for group in range(levels // 4):
+            body(group, 0)
 
     for field in range(FIELDS):
         write(field, [wet[k] * x for k, x in enumerate(read(field))])
@@ -662,8 +680,6 @@
     own = columns // TILE
 
     edge_rows = (species + 1) * (levels * total_lat // LANES) * HALO + 2 * HALO
-    forward = [(i, (i + 1) % count) for i in range(count)]
-    backward = [(b, a) for a, b in forward]
     kinds = rate_table.shape[0]
     roomy = pltpu.CompilerParams(vmem_limit_bytes=GRANT)
     ocean_state, bottom, tracers, land_sea, biome_id, rate_table = placed(
@@ -672,44 +688,64 @@
     vmem = pl.BlockSpec(memory_space=pltpu.VMEM)
     hbm = pl.BlockSpec(memory_space=pltpu.HBM)
 
-    packed, to_west, to_east = pl.pallas_call(
+    pairs = [(i, i ^ 1) for i in range(count)]
+    others = [((a + 1) % count, (b + 1) % count) for a, b in pairs]
+    sizes = (levels, species, total_lat, columns, kinds)
+    edge_shape = (species, levels, TILE, total_lat)
+
+    packed, to_first, to_second = pl.pallas_call(
         pack,
-        out_shape=[far(count * (own + 1) * TILE, LANES), far(edge_rows, LANES), far(edge_rows, LANES)],
+        out_shape=[far(count * (own + 1) * TILE, LANES), near(edge_rows, LANES), near(edge_rows, LANES)],
         in_specs=[hbm] * 5,
-        out_specs=[vmem] * 3,
-        scratch_shapes=grids((LANES, total_lon), (TILE, total_lon))
-        + [pltpu.VMEM(x.shape, x.dtype) for x in (ocean_state, bottom, tracers, land_sea, biome_id)]
-        + [pltpu.SemaphoreType.DMA((5,))],
+        out_specs=[hbm, vmem, vmem],
+        scratch_shapes=grids((LANES, total_lon), (TILE, total_lon), ocean_state.shape)
+        + [pltpu.VMEM(bottom.shape, bottom.dtype)]
+        + grids(edge_shape, edge_shape)
+        + [pltpu.VMEM(x.shape, x.dtype) for x in (land_sea, biome_id)]
+        + grids((count * (own + 1) * TILE, LANES))
+        + [pltpu.SemaphoreType.DMA((6,)), pltpu.SemaphoreType.DMA],
         compiler_params=roomy,
         name="pack",
     )(ocean_state, bottom, tracers, land_sea, biome_id)
-    from_west = lax.ppermute(to_east, "lat", forward)
-    from_east = lax.ppermute(to_west, "lat", backward)
     received = lax.all_to_all(
         packed.reshape(count, (own + 1) * TILE, LANES), "lat", split_axis=0, concat_axis=0, tiled=True
     ).reshape(packed.shape)
-    from_west, from_east, received = placed(pltpu.VMEM, from_west, from_east, received)
-
-    now, wet, biomes, pieces, first = pl.pallas_call(
-        prepare_from,
+    from_first = lax.ppermute(to_first, "lat", pairs)
+    from_second = lax.ppermute(to_second, "lat", others)
+    from_first, from_second, received = placed(pltpu.VMEM, from_first, from_second, received)
+
+    inside = pl.pallas_call(
+        prepare_own,
         out_shape=[
             near(size, LANES),
             near(cells, LANES),
             near(TILE, LANES),
             near(kinds * species, 3 * species, dtype=jnp.bfloat16),
-            near(size, LANES),
         ],
-        in_specs=[hbm] * 4 + [vmem] * 2,
-        out_specs=[vmem] * 5,
+        in_specs=[hbm] * 4,
+        out_specs=[vmem] * 4,
         scratch_shapes=[pltpu.VMEM(x.shape, x.dtype) for x in (tracers, land_sea, biome_id, rate_table)]
-        + grids((cells, LANES))
         + [pltpu.SemaphoreType.DMA((4,))],
         compiler_params=roomy,
+        name="prepare_own",
+    )(tracers, land_sea, biome_id, rate_table)
+    pieces = inside[3]
+
+    def prepare(*refs):
+        prepare_all(*refs, sizes)
+
+    now, wet, biomes, first = pl.pallas_call(
+        prepare,
+        out_shape=[near(size, LANES), near(cells, LANES), near(TILE, LANES), near(size, LANES)],
+        in_specs=[vmem] * 6,
+        out_specs=[vmem] * 4,
+        scratch_shapes=grids((cells, LANES)),
+        compiler_params=roomy,
         name="prepare",
-    )(tracers, land_sea, biome_id, rate_table, from_west, from_east)
+    )(*inside, from_first, from_second)
 
     def run(*refs):
-        advance(*refs, (levels, species, total_lat, columns, kinds))
+        advance(*refs, sizes)
 
     sent, last = pl.pallas_call(
         run,

time: 49.6 us -> 44.1 us (0.89)
  waiting for transfers between devices: 12.5 us -> 9.57 us
  Pallas kernels: 20.6 us -> 17.7 us
    ppermute x2, waiting for transfers between devices: 7.06 us -> 4.15 us  [the longest x1 4.14 us: shards(): from_second = lax.ppermute(to_second, 'lat', others)]
    pallas_call x1, Pallas kernels: 9.13 us -> 7.26 us  [shards(): pl.pallas_call(run, out_shape=[far(count * own * TILE, LANES), far(size,...]
    pallas_call x2 -> x3, Pallas kernels: 7.05 us -> 6.04 us  [the longest x1 2.64 us: shards(): pl.pallas_call(prepare_own, out_shape=[near(size, LANES), near(cells, LAN...]
  transfers between devices with their start and end apart: 4 -> 4, of which waited for: 2 -> 2; matrix products, arithmetic and copies ran while one was open for 0% -> 0% of each run, Pallas kernels for 15% -> 17%
where the time goes in v2:
time: 44.1 us; the launch traced here: 43.7 us
  Pallas kernels  17.7 us (40%)
  starting transfers between devices  15.7 us (36%)
  waiting for transfers between devices  9.57 us (22%)
  between operations  0.69 us (2%)
    all_to_all x1, starting transfers between devices, shards(): lax.all_to_all(packed.reshape(count, (own + 1) * TILE, LANES), 'lat', spl...  7.43 us
    pallas_call x1, Pallas kernels, shards(): pl.pallas_call(run, out_shape=[far(count * own * TILE, LANES), far(size,...  7.26 us
    all_to_all x1, waiting for transfers between devices, shards(): lax.all_to_all(sent.reshape(count, own * TILE, LANES), 'lat', split_axis=...  5.42 us
    ppermute x1, starting transfers between devices, shards(): from_second = lax.ppermute(to_second, 'lat', others)  4.33 us
    ppermute x1, waiting for transfers between devices, shards(): from_second = lax.ppermute(to_second, 'lat', others)  4.14 us
    all_to_all x1, starting transfers between devices, shards(): lax.all_to_all(sent.reshape(count, own * TILE, LANES), 'lat', split_axis=...  3.53 us
    pallas_call x1, Pallas kernels, shards(): pl.pallas_call(unpack_tracers, out_shape=far(*tracers.shape), name='unpac...  3.51 us
    pallas_call x1, Pallas kernels, shards(): pl.pallas_call(prepare_own, out_shape=[near(size, LANES), near(cells, LAN...  2.64 us
  transfers between devices with their start and end apart: 4, of which 2 were waited for; matrix products, arithmetic and copies ran while one was open for 0% of the time, Pallas kernels for 17%

profile of v2, /device:TPU:0, one launch (start us, length us, event | category | flops | bytes accessed | tf_op | source)
XLA Modules:
  0.0 43.7 jit_solution(16951666027233578009)
XLA Ops:
  0.6 2.1 %pack.1 = (f32[512,128]{1,0:T(8,128)}, f32[280,128]{1,0:T(8,128)S(1)}, f32[280,128]{1,0:T(8,128)S(1)}) custom-call(f32[4,16,2,384]{3,2,1,0:T(2,128)} %ocean.1, s32[2,384]{1,0:T(2,128)} %bottom.1, f32[16,16,24,32]{3,2,1,0:T(8,128)} %tracers.3, s32[16,24,32]{2,1,0:T(8,128)} %sea.3, s32[24,32]{1,0:T(8,128)} %biome.3), custom_call_target="tpu_custom_call" | custom-call | tf_op jit(solution)/shard_map/pack/pallas_call | solution.py:696
  2.7 7.4 %all-to-all-start = ((f32[16,32,128]{2,1,0:T(8,128)}), f32[16,32,128]{2,1,0:T(8,128)S(1)}, u32[]{:S(2)}, u32[]{:S(2)}) async-start(f32[16,32,128]{2,1,0:T(8,128)} %bitcast.6), calls=%async_computation | async-start | bytes 524288 | tf_op jit(solution)/shard_map/all_to_all | solution.py:710
  10.1 0.4 collective-permute-start
  10.5 4.3 %collective-permute-start.1 = (f32[280,128]{1,0:T(8,128)S(1)}, f32[280,128]{1,0:T(8,128)S(1)}, u32[]{:S(2)}, u32[]{:S(2)}) collective-permute-start(f32[280,128]{1,0:T(8,128)S(1)} %get-tuple-element.21), channel_id=1, source_target_pairs={{1,2},{2,1},{3,4},{4,3},{5,6},{6,5},{7,8},{8,7},{9,10},{10,9},{11,... | collective-permute-start | bytes 430088 | tf_op jit(solution)/shard_map/ppermute | solution.py:714
  14.9 2.6 %prepare_own.1 = (f32[2048,128]{1,0:T(8,128)S(1)}, f32[128,128]{1,0:T(8,128)S(1)}, f32[8,128]{1,0:T(8,128)S(1)}, bf16[64,48]{1,0:T(8,128)(2,1)S(1)}) custom-call(f32[16,16,24,32]{3,2,1,0:T(8,128)} %tracers.3, s32[16,24,32]{2,1,0:T(8,128)} %sea.3, s32[24,32]{1,0:T(8,128)} %biome.3, f32[4,16,16]{2,1,0:T(8,128)} %rate_table.1), custom_call_target="tpu_custom_call" | custom-call | tf_op jit(solution)/shard_map/prepare_own/pallas_call | solution.py:717
  17.5 0.0 collective-permute-done.refs_4_
  17.5 4.1 %collective-permute-done.1.refs_5_ = f32[280,128]{1,0:T(8,128)S(1)} collective-permute-done((f32[280,128]{1,0:T(8,128)S(1)}, f32[280,128]{1,0:T(8,128)S(1)}, u32[]{:S(2)}, u32[]{:S(2)}) %collective-permute-start.1) | collective-permute-done | bytes 143392 | tf_op jit(solution)/shard_map/ppermute | solution.py:714
  21.7 1.3 %prepare.1 = (f32[2048,128]{1,0:T(8,128)S(1)}, f32[128,128]{1,0:T(8,128)S(1)}, f32[8,128]{1,0:T(8,128)S(1)}, f32[2048,128]{1,0:T(8,128)S(1)}) custom-call(f32[2048,128]{1,0:T(8,128)S(1)} %get-tuple-element.16.refs_0_, f32[128,128]{1,0:T(8,128)S(1)} %get-tuple-element.17.refs_1_, f32[8,128]{1,0:T(8,128)S(1)} %get-tuple-element.18.refs_2_, ...), custom_call_target="tpu_custom_call" | custom-call | tf_op jit(solution)/shard_map/prepare/pallas_call | solution.py:737
  23.0 0.0 all-to-all-done
  23.0 7.3 %advance.1 = (f32[384,128]{1,0:T(8,128)}, f32[2048,128]{1,0:T(8,128)}) custom-call(f32[512,128]{1,0:T(8,128)S(1)} %bitcast.4, f32[2048,128]{1,0:T(8,128)S(1)} %get-tuple-element.22.refs_1_, f32[128,128]{1,0:T(8,128)S(1)} %get-tuple-element.23.refs_2_, f32[8,128]{1,0:T(8,128)S(1)} %get-tuple-element.24.refs_3_, ...), custom_call_target="tpu_custom_call" | custom-call | tf_op jit(solution)/shard_map/advance/pallas_call | solution.py:750
  30.3 3.5 %all-to-all-start.1 = ((f32[16,24,128]{2,1,0:T(8,128)}), f32[16,24,128]{2,1,0:T(8,128)S(1)}, u32[]{:S(2)}, u32[]{:S(2)}) async-start(f32[16,24,128]{2,1,0:T(8,128)} %bitcast.7), calls=%async_computation.1 | async-start | bytes 393216 | tf_op jit(solution)/shard_map/all_to_all | solution.py:768
  33.8 3.5 %unpack_tracers.1 = f32[16,16,24,32]{3,2,1,0:T(8,128)} custom-call(f32[2048,128]{1,0:T(8,128)} %get-tuple-element.27.last_ref), custom_call_target="tpu_custom_call" | custom-call | tf_op jit(solution)/shard_map/unpack_tracers/pallas_call | solution.py:773
  37.4 5.4 %all-to-all-done.1 = f32[16,24,128]{2,1,0:T(8,128)S(1)} async-done(((f32[16,24,128]{2,1,0:T(8,128)}), f32[16,24,128]{2,1,0:T(8,128)S(1)}, u32[]{:S(2)}, u32[]{:S(2)}) %all-to-all-start.1) | async-done | bytes 196640 | tf_op jit(solution)/shard_map/all_to_all | solution.py:768
  42.8 0.9 %unpack_ocean.1 = f32[4,16,2,384]{3,2,1,0:T(2,128)} custom-call(f32[384,128]{1,0:T(8,128)S(1)} %bitcast.5), custom_call_target="tpu_custom_call" | custom-call | tf_op jit(solution)/shard_map/unpack_ocean/pallas_call | solution.py:776
Async XLA Ops:
  2.7 20.3 %all-to-all-start = ((f32[16,32,128]{2,1,0:T(8,128)}), f32[16,32,128]{2,1,0:T(8,128)S(1)}, u32[]{:S(2)}, u32[]{:S(2)}) async-start(f32[16,32,128]{2,1,0:T(8,128)} %bitcast.6), calls=%async_computation | async-start | bytes 524288 | tf_op jit(solution)/shard_map/all_to_all | solution.py:710
  10.1 7.4 %collective-permute-start = (f32[280,128]{1,0:T(8,128)S(1)}, f32[280,128]{1,0:T(8,128)S(1)}, u32[]{:S(2)}, u32[]{:S(2)}) collective-permute-start(f32[280,128]{1,0:T(8,128)S(1)} %get-tuple-element.20), channel_id=1, source_target_pairs={{0,1},{1,0},{2,3},{3,2},{4,5},{5,4},{6,7},{7,6},{8,9},{9,8},{10,11... | collective-permute-start | bytes 430088 | tf_op jit(solution)/shard_map/ppermute | solution.py:713
  10.5 11.1 %collective-permute-start.1 = (f32[280,128]{1,0:T(8,128)S(1)}, f32[280,128]{1,0:T(8,128)S(1)}, u32[]{:S(2)}, u32[]{:S(2)}) collective-permute-start(f32[280,128]{1,0:T(8,128)S(1)} %get-tuple-element.21), channel_id=1, source_target_pairs={{1,2},{2,1},{3,4},{4,3},{5,6},{6,5},{7,8},{8,7},{9,10},{10,9},{11,... | collective-permute-start | bytes 430088 | tf_op jit(solution)/shard_map/ppermute | solution.py:714
  30.3 12.5 %all-to-all-start.1 = ((f32[16,24,128]{2,1,0:T(8,128)}), f32[16,24,128]{2,1,0:T(8,128)S(1)}, u32[]{:S(2)}, u32[]{:S(2)}) async-start(f32[16,24,128]{2,1,0:T(8,128)} %bitcast.7), calls=%async_computation.1 | async-start | bytes 393216 | tf_op jit(solution)/shard_map/all_to_all | solution.py:768

commit v3 on v2

--- a/solution.py
+++ b/solution.py
@@ -438,12 +438,13 @@
         chosen = biome_masks(biomes_ref, row, kinds, species)
         every = list(range(levels))
         for level, change in zip(every, reaction(now_ref, 0, pieces, chosen, growth, row, every, species), strict=True):
-            first_ref[pl.ds((level * TILE + row) * species, species), :] = change
+            mask = wet_ref[pl.ds(level * TILE + row, species, stride=0), :]
+            first_ref[pl.ds((level * TILE + row) * species, species), :] = mask * change
 
 
 def advance(
-    received, now_ref, wet_ref, biomes_ref, pieces_ref, first_ref, sent_out, last_out, sent, last_ref, work, ocean, coef,
-    tracer, growth, done, sizes,
+    received, now_ref, wet_ref, biomes_ref, pieces_ref, first_ref, sent_out, last_ref, sent, work, ocean, coef, tracer, growth,
+    done, sizes,
 ):
     levels, species, total_lat, columns, kinds = sizes
     pieces = pieces_ref[...]
@@ -569,7 +570,7 @@
                     above = max(level - 1, 0) * TILE + r
                     under = min(level + 1, levels - 1) * TILE + r
                     weight = [coef[pl.ds(start + i * plane + cell, species, stride=0), :] for i in range(7)]
-                    mask = wet_ref[pl.ds(cell, species, stride=0), :]
+                    mask = None if ready is not None else wet_ref[pl.ds(cell, species, stride=0), :]
 
                     def take(index):
                         return source[pl.ds(base + index * species, species), :]
@@ -577,12 +578,12 @@
                     x = take(cell)
                     x_east = take(cell + 1) if r < TILE - 1 else spin(take(cell - r), -total_lat, 1)
                     x_west = take(cell - 1) if r > 0 else spin(take(cell + TILE - 1), total_lat, 1)
-                    change = sums[place] if ready is None else ready[pl.ds(cell * species, species), :]
+                    change = mask * sums[place] if ready is None else ready[pl.ds(cell * species, species), :]
                     value = (
                         (weight[0] * x + weight[1] * x_east)
                         + (weight[2] * x_west + weight[3] * spin(x, -1, 1))
                         + (weight[4] * spin(x, 1, 1) + weight[5] * take(above))
-                        + (weight[6] * take(under) + mask * change)
+                        + (weight[6] * take(under) + change)
                     )
                     target[pl.ds(target_base + cell * species, species), :] = value
             return carry
@@ -605,9 +606,6 @@
                 put_growth(growth, source, levels, species, total_lat, base)
             substep(step, source, base, target, target_base, first_ref if first else None)
             source, base = target, target_base
-        if step == STEPS - 1:
-            keep = pltpu.make_async_copy(last_ref, last_out, done.at[0])
-            keep.start()
         lit = light(planes_of(source, 0, levels, species, base), surface_light(total_lat))
         warm = []
         for k, x in enumerate(read(2)):
@@ -626,10 +624,9 @@
                 sent[pl.ds(q * TILE + j * 4 + r_low, count, stride=own * TILE), :] = work[
                     pl.ds(r_low * LANES + q * total_lat + j, count, stride=2), :
                 ]
-    send = pltpu.make_async_copy(sent, sent_out, done.at[1])
+    send = pltpu.make_async_copy(sent, sent_out, done)
     send.start()
     send.wait()
-    keep.wait()
 
 
 def unpack_tracers(last_ref, out_ref):
@@ -749,29 +746,33 @@
 
     sent, last = pl.pallas_call(
         run,
-        out_shape=[far(count * own * TILE, LANES), far(size, LANES)],
+        out_shape=[far(count * own * TILE, LANES), near(size, LANES)],
         in_specs=[vmem] * 6,
-        out_specs=[hbm] * 2,
+        out_specs=[hbm, vmem],
         scratch_shapes=grids(
             (count * own * TILE, LANES),
-            (size, LANES),
             (4 * LANES, LANES),
             (FIELDS * cells, LANES),
             (STEPS * 7 * cells, LANES),
             (2 * size, LANES),
             (cells, LANES),
         )
-        + [pltpu.SemaphoreType.DMA((2,))],
-        compiler_params=roomy,
+        + [pltpu.SemaphoreType.DMA],
+        compiler_params=pltpu.CompilerParams(vmem_limit_bytes=GRANT),
         name="advance",
     )(received, now, wet, biomes, pieces, first)
     back = lax.all_to_all(
         sent.reshape(count, own * TILE, LANES), "lat", split_axis=0, concat_axis=0, tiled=True
     ).reshape(sent.shape)
     (back,) = placed(pltpu.VMEM, back)
-    (last,) = placed(pltpu.HBM, last)
+    (last,) = placed(pltpu.VMEM, last)
     tracers_out = pl.pallas_call(
-        unpack_tracers, out_shape=far(*tracers.shape), name="unpack_tracers"
+        unpack_tracers,
+        out_shape=far(*tracers.shape),
+        in_specs=[vmem],
+        out_specs=vmem,
+        compiler_params=roomy,
+        name="unpack_tracers",
     )(last)
     state_out = pl.pallas_call(
         unpack_ocean,

time: 44.1 us -> 43.9 us (level)
  Pallas kernels: 17.7 us -> 16.3 us
  waiting for transfers between devices: 9.57 us -> 10.8 us
    pallas_call x2, Pallas kernels: 10.8 us -> 9.33 us  [the longest x1 7.05 us: shards(): pl.pallas_call(run, out_shape=[far(count * own * TILE, LANES), near(size,...]
    all_to_all x1, waiting for transfers between devices: 5.42 us -> 6.64 us  [shards(): lax.all_to_all(sent.reshape(count, own * TILE, LANES), 'lat', split_axis=...]
  transfers between devices with their start and end apart: 4 -> 4, of which waited for: 2 -> 2; matrix products, arithmetic and copies ran while one was open for 0% -> 0% of each run, Pallas kernels for 17% -> 14%
where the time goes in v3:
time: 43.9 us; the launch traced here: 43.5 us
  Pallas kernels  16.3 us (37%)
  starting transfers between devices  15.7 us (36%)
  waiting for transfers between devices  10.8 us (25%)
  between operations  0.7 us (2%)
    all_to_all x1, starting transfers between devices, shards(): lax.all_to_all(packed.reshape(count, (own + 1) * TILE, LANES), 'lat', spl...  7.43 us
    pallas_call x1, Pallas kernels, shards(): pl.pallas_call(run, out_shape=[far(count * own * TILE, LANES), near(size,...  7.05 us
    all_to_all x1, waiting for transfers between devices, shards(): lax.all_to_all(sent.reshape(count, own * TILE, LANES), 'lat', split_axis=...  6.64 us
    ppermute x1, starting transfers between devices, shards(): from_second = lax.ppermute(to_second, 'lat', others)  4.33 us
    ppermute x1, waiting for transfers between devices, shards(): from_second = lax.ppermute(to_second, 'lat', others)  4.14 us
    all_to_all x1, starting transfers between devices, shards(): lax.all_to_all(sent.reshape(count, own * TILE, LANES), 'lat', split_axis=...  3.53 us
    pallas_call x1, Pallas kernels, shards(): pl.pallas_call(prepare_own, out_shape=[near(size, LANES), near(cells, LAN...  2.64 us
    pallas_call x1, Pallas kernels, shards(): pl.pallas_call(unpack_tracers, out_shape=far(*tracers.shape), in_specs=[v...  2.28 us
  transfers between devices with their start and end apart: 4, of which 2 were waited for; matrix products, arithmetic and copies ran while one was open for 0% of the time, Pallas kernels for 14%

profile of v3, /device:TPU:0, one launch (start us, length us, event | category | flops | bytes accessed | tf_op | source)
XLA Modules:
  0.0 43.5 jit_solution(15450723504781109312)
XLA Ops:
  0.6 2.1 %pack.1 = (f32[512,128]{1,0:T(8,128)}, f32[280,128]{1,0:T(8,128)S(1)}, f32[280,128]{1,0:T(8,128)S(1)}) custom-call(f32[4,16,2,384]{3,2,1,0:T(2,128)} %ocean.1, s32[2,384]{1,0:T(2,128)} %bottom.1, f32[16,16,24,32]{3,2,1,0:T(8,128)} %tracers.3, s32[16,24,32]{2,1,0:T(8,128)} %sea.3, s32[24,32]{1,0:T(8,128)} %biome.3), custom_call_target="tpu_custom_call" | custom-call | tf_op jit(solution)/shard_map/pack/pallas_call | solution.py:693
  2.7 7.4 %all-to-all-start = ((f32[16,32,128]{2,1,0:T(8,128)}), f32[16,32,128]{2,1,0:T(8,128)S(1)}, u32[]{:S(2)}, u32[]{:S(2)}) async-start(f32[16,32,128]{2,1,0:T(8,128)} %bitcast.6), calls=%async_computation | async-start | bytes 524288 | tf_op jit(solution)/shard_map/all_to_all | solution.py:707
  10.1 0.4 collective-permute-start
  10.5 4.3 %collective-permute-start.1 = (f32[280,128]{1,0:T(8,128)S(1)}, f32[280,128]{1,0:T(8,128)S(1)}, u32[]{:S(2)}, u32[]{:S(2)}) collective-permute-start(f32[280,128]{1,0:T(8,128)S(1)} %get-tuple-element.21), channel_id=1, source_target_pairs={{1,2},{2,1},{3,4},{4,3},{5,6},{6,5},{7,8},{8,7},{9,10},{10,9},{11,... | collective-permute-start | bytes 430088 | tf_op jit(solution)/shard_map/ppermute | solution.py:711
  14.9 2.6 %prepare_own.1 = (f32[2048,128]{1,0:T(8,128)S(1)}, f32[128,128]{1,0:T(8,128)S(1)}, f32[8,128]{1,0:T(8,128)S(1)}, bf16[64,48]{1,0:T(8,128)(2,1)S(1)}) custom-call(f32[16,16,24,32]{3,2,1,0:T(8,128)} %tracers.3, s32[16,24,32]{2,1,0:T(8,128)} %sea.3, s32[24,32]{1,0:T(8,128)} %biome.3, f32[4,16,16]{2,1,0:T(8,128)} %rate_table.1), custom_call_target="tpu_custom_call" | custom-call | tf_op jit(solution)/shard_map/prepare_own/pallas_call | solution.py:714
  17.5 0.0 collective-permute-done.refs_4_
  17.5 4.1 %collective-permute-done.1.refs_5_ = f32[280,128]{1,0:T(8,128)S(1)} collective-permute-done((f32[280,128]{1,0:T(8,128)S(1)}, f32[280,128]{1,0:T(8,128)S(1)}, u32[]{:S(2)}, u32[]{:S(2)}) %collective-permute-start.1) | collective-permute-done | bytes 143392 | tf_op jit(solution)/shard_map/ppermute | solution.py:711
  21.7 1.3 %prepare.1 = (f32[2048,128]{1,0:T(8,128)S(1)}, f32[128,128]{1,0:T(8,128)S(1)}, f32[8,128]{1,0:T(8,128)S(1)}, f32[2048,128]{1,0:T(8,128)S(1)}) custom-call(f32[2048,128]{1,0:T(8,128)S(1)} %get-tuple-element.16.refs_0_, f32[128,128]{1,0:T(8,128)S(1)} %get-tuple-element.17.refs_1_, f32[8,128]{1,0:T(8,128)S(1)} %get-tuple-element.18.refs_2_, ...), custom_call_target="tpu_custom_call" | custom-call | tf_op jit(solution)/shard_map/prepare/pallas_call | solution.py:734
  23.0 0.0 all-to-all-done
  23.0 7.0 %advance.1 = (f32[384,128]{1,0:T(8,128)}, f32[2048,128]{1,0:T(8,128)S(1)}) custom-call(f32[512,128]{1,0:T(8,128)S(1)} %bitcast.4, f32[2048,128]{1,0:T(8,128)S(1)} %get-tuple-element.22.refs_1_, f32[128,128]{1,0:T(8,128)S(1)} %get-tuple-element.23.refs_2_, f32[8,128]{1,0:T(8,128)S(1)} %get-tuple-element.24.refs_3_, ...), custom_call_target="tpu_custom_call" | custom-call | tf_op jit(solution)/shard_map/advance/pallas_call | solution.py:747
  30.1 3.5 %all-to-all-start.1 = ((f32[16,24,128]{2,1,0:T(8,128)}), f32[16,24,128]{2,1,0:T(8,128)S(1)}, u32[]{:S(2)}, u32[]{:S(2)}) async-start(f32[16,24,128]{2,1,0:T(8,128)} %bitcast.7), calls=%async_computation.1 | async-start | bytes 393216 | tf_op jit(solution)/shard_map/all_to_all | solution.py:764
  33.6 2.3 %unpack_tracers.1 = f32[16,16,24,32]{3,2,1,0:T(8,128)} custom-call(f32[2048,128]{1,0:T(8,128)S(1)} %get-tuple-element.27.last_ref), custom_call_target="tpu_custom_call" | custom-call | tf_op jit(solution)/shard_map/unpack_tracers/pallas_call | solution.py:769
  35.9 6.6 %all-to-all-done.1 = f32[16,24,128]{2,1,0:T(8,128)S(1)} async-done(((f32[16,24,128]{2,1,0:T(8,128)}), f32[16,24,128]{2,1,0:T(8,128)S(1)}, u32[]{:S(2)}, u32[]{:S(2)}) %all-to-all-start.1) | async-done | bytes 196640 | tf_op jit(solution)/shard_map/all_to_all | solution.py:764
  42.6 0.9 %unpack_ocean.1 = f32[4,16,2,384]{3,2,1,0:T(2,128)} custom-call(f32[384,128]{1,0:T(8,128)S(1)} %bitcast.5), custom_call_target="tpu_custom_call" | custom-call | tf_op jit(solution)/shard_map/unpack_ocean/pallas_call | solution.py:777
Async XLA Ops:
  2.7 20.3 %all-to-all-start = ((f32[16,32,128]{2,1,0:T(8,128)}), f32[16,32,128]{2,1,0:T(8,128)S(1)}, u32[]{:S(2)}, u32[]{:S(2)}) async-start(f32[16,32,128]{2,1,0:T(8,128)} %bitcast.6), calls=%async_computation | async-start | bytes 524288 | tf_op jit(solution)/shard_map/all_to_all | solution.py:707
  10.1 7.4 %collective-permute-start = (f32[280,128]{1,0:T(8,128)S(1)}, f32[280,128]{1,0:T(8,128)S(1)}, u32[]{:S(2)}, u32[]{:S(2)}) collective-permute-start(f32[280,128]{1,0:T(8,128)S(1)} %get-tuple-element.20), channel_id=1, source_target_pairs={{0,1},{1,0},{2,3},{3,2},{4,5},{5,4},{6,7},{7,6},{8,9},{9,8},{10,11... | collective-permute-start | bytes 430088 | tf_op jit(solution)/shard_map/ppermute | solution.py:710
  10.5 11.1 %collective-permute-start.1 = (f32[280,128]{1,0:T(8,128)S(1)}, f32[280,128]{1,0:T(8,128)S(1)}, u32[]{:S(2)}, u32[]{:S(2)}) collective-permute-start(f32[280,128]{1,0:T(8,128)S(1)} %get-tuple-element.21), channel_id=1, source_target_pairs={{1,2},{2,1},{3,4},{4,3},{5,6},{6,5},{7,8},{8,7},{9,10},{10,9},{11,... | collective-permute-start | bytes 430088 | tf_op jit(solution)/shard_map/ppermute | solution.py:711
  30.1 12.5 %all-to-all-start.1 = ((f32[16,24,128]{2,1,0:T(8,128)}), f32[16,24,128]{2,1,0:T(8,128)S(1)}, u32[]{:S(2)}, u32[]{:S(2)}) async-start(f32[16,24,128]{2,1,0:T(8,128)} %bitcast.7), calls=%async_computation.1 | async-start | bytes 393216 | tf_op jit(solution)/shard_map/all_to_all | solution.py:764

commit v4 on v3

--- a/solution.py
+++ b/solution.py
@@ -185,15 +185,11 @@
         and HALO == TILE // 2
         and lat_rows * lat_count == total_lat
         and columns * lat_count == total_lon
-        and columns % TILE == 0
-        and LANES % total_lat == 0
-        and (columns + 2 * HALO) * total_lat == TILE * LANES
-        and 2 * FIELDS * levels == LANES
-        and levels <= columns + HALO
-        and 2 * columns + 3 * HALO <= FIELDS * levels
+        and columns == 3 * TILE
+        and LANES == 4 * total_lat
+        and levels == 2 * TILE
         and species == 2 * TILE
         and lat_count % 2 == 0
-        and levels % (LANES // total_lat) == 0
     )
 
 
@@ -211,40 +207,74 @@
     return block if amount == 0 else pltpu.roll(block, amount, axis)
 
 
-def swap_halves(block):
-    low_row, low_lane = rows_of() < TILE // 2, lanes_of() < LANES // 2
-    other = spin(spin(block, LANES // 2, 1), TILE // 2, 0)
-    return jnp.where(low_row == low_lane, block, other)
-
-
-def pack_ocean(ocean_ref, bottom_ref, out_ref, flat, depth):
+def pack_ocean(ocean_ref, bottom_ref, own_ref, out_ref, turned, lined):
     fields, levels, lat_rows, total_lon = ocean_ref.shape
     half = fields * levels
-    count = out_ref.shape[0] // (4 * TILE)
+    parts = 3
+    count = out_ref.shape[0] // (parts * TILE)
     columns = total_lon // count
     own = columns // TILE
     for index in range(half):
         field, level = divmod(index, levels)
         for row in range(lat_rows):
-            flat[row * half + index : row * half + index + 1, :] = ocean_ref[field, level, row : row + 1, :]
-    turned = flat[...].T
-    tiles = [turned[TILE * i : TILE * (i + 1), :] for i in range(total_lon // TILE)]
-    swapped = [swap_halves(t) for t in tiles]
-    depth[...] = jnp.zeros(depth.shape, jnp.float32)
-    depth[3:4, :] = bottom_ref[0:1, :].astype(jnp.float32)
-    depth[7:8, :] = bottom_ref[1:2, :].astype(jnp.float32)
-    line = depth[...]
-    row, lane = rows_of(), lanes_of()
-    width = columns + 2 * HALO
-    window = (row % 4 == 3) & (lane >= width - HALO) & (lane < 2 * width - HALO)
-    for target in range(count):
-        for q in range(own):
-            out_ref[pl.ds((target * (own + 1) + q) * TILE, TILE), :] = swapped[target * own + q]
-        east = tiles[(target * own + own) % len(tiles)]
-        west = tiles[target * own - 1]
-        edge = swap_halves(jnp.where(row < HALO, east, west))
-        level_line = spin(line, width - target * columns, 1)[:, :LANES]
-        out_ref[pl.ds((target * (own + 1) + own) * TILE, TILE), :] = jnp.where(window, level_line, edge)
+            own_ref[row * half + index : row * half + index + 1, :] = ocean_ref[field, level, row : row + 1, :]
+    own_ref[2 * half : 2 * half + TILE, :] = jnp.zeros((TILE, total_lon), jnp.float32)
+    for row in range(lat_rows):
+        own_ref[2 * half + row : 2 * half + row + 1, :] = bottom_ref[row : row + 1, :].astype(jnp.float32)
+
+    def rows(row, field):
+        return own_ref[row * half + field * levels : row * half + (field + 1) * levels, :]
+
+    stack = [rows(row, field) for field in range(2) for row in range(lat_rows)]
+    stack += [gravity * (haline_coef * rows(row, 3) - therm_coef * rows(row, 2)) for row in range(lat_rows)]
+    stack.append(jnp.zeros((LANES - 2 * parts * levels, total_lon), jnp.float32))
+    turned[...] = jnp.concatenate(stack, axis=0).T
+    tiles = total_lon // TILE
+    group = lanes_of((tiles, LANES)) // levels
+    joined = [jnp.zeros((tiles, LANES), jnp.float32) for _ in range(parts * lat_rows)]
+    for r in range(TILE):
+        line = turned[pl.ds(r, tiles, stride=TILE), :]
+        joined = [jnp.where(group == r, spin(line, (r - i) * levels, 1), x) for i, x in enumerate(joined)]
+    block = tiles + 2 * TILE
+    for i, x in enumerate(joined):
+        lined[i * block : i * block + TILE, :] = x[tiles - TILE :, :]
+        lined[i * block + TILE : i * block + TILE + tiles, :] = x
+        lined[i * block + TILE + tiles : (i + 1) * block, :] = x[:TILE, :]
+    lane = lanes_of()
+    span = (lane >= 3 * levels) & (lane < 4 * levels)
+    index = rows_of()
+    for row in range(lat_rows):
+        floor = jnp.broadcast_to(own_ref[2 * half + row : 2 * half + row + 1, :], (TILE, total_lon))
+        lines = {1: [], 2: []}
+        for start in range(0, count, TILE):
+            near_ones = jnp.zeros((TILE, LANES), jnp.float32)
+            far_ones = near_ones
+            for i in range(TILE):
+                first = (start + i) * columns
+                inner = spin(floor, 3 * levels - first, 1)[:, :LANES]
+                outer = spin(floor, 2 * levels - first, 1)[:, :LANES]
+                wrap = spin(floor, 4 * levels - first, 1)[:, :LANES]
+                near_ones = jnp.where(index == i, inner, near_ones)
+                far_ones = jnp.where(index == i, jnp.where(lane < 4 * levels - HALO, outer, wrap), far_ones)
+            lines[1].append(near_ones)
+            lines[2].append(far_ones)
+        for part in range(parts):
+            base = (part * lat_rows + row) * block + TILE
+            for q in range(own):
+                out_ref[pl.ds(part * TILE + q * 2 + row, count, stride=parts * TILE), :] = lined[
+                    pl.ds(base + q, count, stride=own), :
+                ]
+            lane_all = lanes_of((count, LANES))
+            edge = jnp.where(
+                lane_all < HALO * levels,
+                lined[pl.ds(base + own, count, stride=own), :],
+                lined[pl.ds(base - 1, count, stride=own), :],
+            )
+            if part > 0:
+                edge = jnp.concatenate(
+                    [jnp.where(span, lines[part][i], edge[TILE * i : TILE * (i + 1), :]) for i in range(count // TILE)], axis=0
+                )
+            out_ref[pl.ds(part * TILE + own * 2 + row, count, stride=parts * TILE), :] = edge
 
 
 def pack_edges(low_ref, high_ref, sea_ref, biome_ref, first_ref, second_ref, even):
@@ -295,19 +325,20 @@
 
 
 def pack(ocean, bottom, tracers, sea, biome, *refs):
-    out, edges, (flat, depth), held, result, ready, gone = refs[0], refs[1:3], refs[3:5], refs[5:11], refs[11], refs[12], refs[13]
+    out, edges, home_out, (turned, lined), held = refs[0], refs[1:3], refs[3], refs[4:6], refs[6:12]
+    result, home, ready, gone = refs[12:16]
     columns = tracers.shape[2]
     sources = [ocean, bottom, tracers.at[:, :, 0:TILE, :], tracers.at[:, :, columns - TILE : columns, :], sea, biome]
     copies = fetch(sources, held, ready)
     copies[0].wait()
     copies[1].wait()
-    pack_ocean(held[0], held[1], result, flat, depth)
-    leaving = pltpu.make_async_copy(result, out, gone)
-    leaving.start()
+    pack_ocean(held[0], held[1], home, result, turned, lined)
+    leaving = fetch([result, home], [out, home_out], gone)
     for copy in copies[2:]:
         copy.wait()
     pack_edges(*held[2:], *edges, is_even())
-    leaving.wait()
+    for copy in leaving:
+        copy.wait()
 
 
 def light(plankton, surface):
@@ -444,32 +475,27 @@
 
 def advance(
     received, now_ref, wet_ref, biomes_ref, pieces_ref, first_ref, sent_out, last_ref, sent, work, ocean, coef, tracer, growth,
-    done, sizes,
+    heat, done, sizes,
 ):
     levels, species, total_lat, columns, kinds = sizes
     pieces = pieces_ref[...]
     count = total_lat // 2
     own = columns // TILE
-    half = FIELDS * levels
     row, lane = rows_of(), lanes_of()
     lat = lane % total_lat
-    width = columns + 2 * HALO
-
-    for r_low in range(4):
+
+    turned = []
+    for part in range(3):
         for q in range(own + 1):
             for j in range(2):
-                work[pl.ds(r_low * LANES + q * total_lat + j, count, stride=2), :] = received[
-                    pl.ds(q * TILE + j * 4 + r_low, count, stride=(own + 1) * TILE), :
+                work[pl.ds(part * LANES + q * total_lat + j, count, stride=2), :] = received[
+                    pl.ds(part * TILE + q * 2 + j, count, stride=3 * TILE), :
                 ]
-    turned = None
-    for r_low in range(4):
-        turned = work[r_low * LANES : (r_low + 1) * LANES, :].T
-        for r_high in range(2):
-            ocean[pl.ds(r_high * 4 + r_low, half, stride=TILE), :] = turned[r_high * half : (r_high + 1) * half, :]
-    floors = [turned[width + TILE * q : width + TILE * (q + 1), :] for q in range(own)]
-    floors.append(
-        jnp.where(row < HALO, turned[width + columns : width + columns + TILE, :], turned[width - TILE : width, :])
-    )
+        turned.append(work[part * LANES : (part + 1) * LANES, :].T)
+        for r in range(TILE):
+            ocean[pl.ds(part * levels * TILE + r, levels, stride=TILE), :] = turned[part][r * levels : (r + 1) * levels, :]
+    spare = 3 * levels
+    floors = [turned[1 + q // 2][spare + q % 2 * TILE : spare + (q % 2 + 1) * TILE, :] for q in range(own + 1)]
     floor = floors[own]
     for q in range(own):
         floor = jnp.where(lane // total_lat == q, spin(floors[q], (q - own) * total_lat, 1), floor)
@@ -501,20 +527,20 @@
     plane = levels * TILE
 
     def dynamics(step):
-        speed_u, speed_v, temper, salty = read(0), read(1), read(2), read(3)
+        speed_u, speed_v, steps = read(0), read(1), read(2)
         spread, new_u, new_v = [], [], []
         pressure = None
         for k in range(levels):
             u, v = speed_u[k], speed_v[k]
-            part = gravity * (haline_coef * salty[k] - therm_coef * temper[k])
-            pressure = part if pressure is None else pressure + part
-            slope_east = 0.5 * (east(pressure) - west(pressure))
-            slope_north = 0.5 * (north(pressure) - south(pressure))
             u_east, u_west, v_north, v_south = east(u), west(u), north(v), south(v)
-            lap_u = u_east + u_west + north(u) + south(u) - 4.0 * u
-            lap_v = east(v) + west(v) + v_north + v_south - 4.0 * v
-            new_u.append(wet[k] * (u + time_step * (spin_rate * v - slope_east + viscosity * lap_u)))
-            new_v.append(wet[k] * (v + time_step * (-spin_rate * u - slope_north + viscosity * lap_v)))
+            if step < STEPS - 1:
+                pressure = steps[k] if pressure is None else pressure + steps[k]
+                slope_east = 0.5 * (east(pressure) - west(pressure))
+                slope_north = 0.5 * (north(pressure) - south(pressure))
+                lap_u = u_east + u_west + north(u) + south(u) - 4.0 * u
+                lap_v = east(v) + west(v) + v_north + v_south - 4.0 * v
+                new_u.append(wet[k] * (u + time_step * (spin_rate * v - slope_east + viscosity * lap_u)))
+                new_v.append(wet[k] * (v + time_step * (-spin_rate * u - slope_north + viscosity * lap_v)))
             spread.append(0.5 * (u_east - u_west) + 0.5 * (v_north - v_south))
             face_east = 0.5 * (u + u_east)
             face_west = west(face_east)
@@ -545,16 +571,9 @@
             coef[pl.ds(at + 5 * plane, TILE), :] = -mask * down
             coef[pl.ds(at + 6 * plane, TILE), :] = mask * below_up
             below_up, below_down = up, down
-        for field, values, rate in ((2, temper, heat_diff), (3, salty, salt_diff)):
-            fresh = []
-            for k in range(levels):
-                x = values[k]
-                lap = east(x) + west(x) + north(x) + south(x) - 4.0 * x
-                y = x + time_step * rate * lap
-                fresh.append(wet[k] * y if field == 3 else y)
-            write(field, fresh)
-        write(0, new_u)
-        write(1, new_v)
+        if step < STEPS - 1:
+            write(0, new_u)
+            write(1, new_v)
 
     def substep(step, source, base, target, target_base, ready):
         start = step * 7 * plane
@@ -591,7 +610,7 @@
         for group in range(levels // 4):
             body(group, 0)
 
-    for field in range(FIELDS):
+    for field in range(3):
         write(field, [wet[k] * x for k, x in enumerate(read(field))])
     size = levels * TILE * species
     source, base = now_ref, 0
@@ -607,23 +626,23 @@
             substep(step, source, base, target, target_base, first_ref if first else None)
             source, base = target, target_base
         lit = light(planes_of(source, 0, levels, species, base), surface_light(total_lat))
-        warm = []
-        for k, x in enumerate(read(2)):
+        for k in range(levels):
             _, top_light, attenuate = lit[k]
             heating = heat_gain * sea[k] * (top_light * (1.0 - jnp.exp(-attenuate)))
-            warm.append(wet[k] * (x + time_step * heating))
-        write(2, warm)
-
-    for r_low in range(4):
-        both = jnp.concatenate(
-            [ocean[pl.ds(r_high * 4 + r_low, half, stride=TILE), :] for r_high in range(2)], axis=0
-        )
-        work[r_low * LANES : (r_low + 1) * LANES, :] = both.T
+            for place, shift in enumerate(range(-1, 3) if step < STEPS - 1 else range(2)):
+                at = ((place + 4 * step) * levels + k) * TILE
+                heat[at : at + TILE, :] = spin(heating, -shift, 1)
+
+    kinds_of_row = 6 * levels
+    blank = jnp.zeros((LANES - kinds_of_row, LANES), jnp.float32)
+    for r in range(TILE):
+        work[r * LANES : (r + 1) * LANES, :] = jnp.concatenate(
+            [heat[pl.ds(r, kinds_of_row, stride=TILE), :], blank], axis=0
+        ).T
         for q in range(own):
-            for j in range(2):
-                sent[pl.ds(q * TILE + j * 4 + r_low, count, stride=own * TILE), :] = work[
-                    pl.ds(r_low * LANES + q * total_lat + j, count, stride=2), :
-                ]
+            sent[pl.ds(q * TILE + r, count, stride=own * TILE), :] = work[
+                pl.ds(r * LANES + q * total_lat, count, stride=2), :
+            ]
     send = pltpu.make_async_copy(sent, sent_out, done)
     send.start()
     send.wait()
@@ -638,15 +657,91 @@
                 out_ref[kind, level, TILE * q : TILE * (q + 1), :] = whole[:, q * total_lat : (q + 1) * total_lat]
 
 
-def unpack_ocean(received, out_ref, turned, flat):
-    fields, levels, lat_rows, total_lon = out_ref.shape
+def down_sum(x):
+    index = rows_of(x.shape)
+    step = 1
+    while step < x.shape[0]:
+        x = x + jnp.where(index >= step, spin(x, step, 0), 0.0)
+        step *= 2
+    return x
+
+
+def slope(x):
+    return 0.5 * (spin(x, -1, 1) - spin(x, 1, 1))
+
+
+def lap(before, x, after):
+    return spin(x, -1, 1) + spin(x, 1, 1) + after + before - 4.0 * x
+
+
+def at_home(own_ref, first_ref, second_ref, base_ref, wet_ref, levels, total_lat):
+    half = FIELDS * levels
+    rows = range(-2, 4)
+    start = lax.axis_index("lat") * 2
+    even = is_even()
+
+    def raw(at, size, offset):
+        place = slice(at % 2 * offset[0] + offset[1], at % 2 * offset[0] + offset[1] + size)
+        if 0 <= at < 2:
+            return own_ref[place, :]
+        return jnp.where(even == (at > 0), first_ref[place, :], second_ref[place, :])
+
+    wet, u, v, t, s = {}, {}, {}, {}, {}
+    for j in rows:
+        floor = raw(j, 1, (1, 2 * half))
+        level = rows_of((levels, floor.shape[1])).astype(jnp.float32)
+        wet[j] = (level < floor).astype(jnp.float32)
+        u[j], v[j], t[j], s[j] = [wet[j] * raw(j, levels, (half, field * levels)) for field in range(FIELDS)]
+
+    def step(u, v, t, s, inner):
+        pressure = {j: gravity * down_sum(haline_coef * s[j] - therm_coef * t[j]) for j in u}
+        fresh = ({}, {}, {}, {})
+        for j in inner:
+            turn = coriolis * (2.0 * ((start + j).astype(jnp.float32) + 0.5) / total_lat - 1.0)
+            north_slope = 0.5 * (pressure[j + 1] - pressure[j - 1])
+            laps = [lap(x[j - 1], x[j], x[j + 1]) for x in (u, v, t, s)]
+            fresh[0][j] = wet[j] * (u[j] + time_step * (turn * v[j] - slope(pressure[j]) + viscosity * laps[0]))
+            fresh[1][j] = wet[j] * (v[j] + time_step * (-turn * u[j] - north_slope + viscosity * laps[1]))
+            fresh[2][j] = wet[j] * (t[j] + time_step * heat_diff * laps[2])
+            fresh[3][j] = wet[j] * (s[j] + time_step * salt_diff * laps[3])
+        return fresh
+
+    final = step(*step(u, v, t, s, range(-1, 3)), range(2))
+    for j in range(2):
+        for field in range(FIELDS):
+            begin = j * half + field * levels
+            base_ref[begin : begin + levels, :] = final[field][j]
+    for j in range(-1, 3):
+        wet_ref[(j + 1) * levels : (j + 2) * levels, :] = wet[j]
+
+
+def finish(received, base_ref, wet_ref, out_ref, flat):
+    fields, levels, _, _ = out_ref.shape
     half = fields * levels
-    for i in range(total_lon // TILE):
-        turned[TILE * i : TILE * (i + 1), :] = swap_halves(received[TILE * i : TILE * (i + 1), :])
-    flat[...] = turned[...].T
+    heating = received[...].T
+
+    def part(ref, place):
+        return ref[place * levels : (place + 1) * levels, :]
+
+    wet = {j: part(wet_ref, j + 1) for j in range(-1, 3)}
+    warm = {j: time_step * (wet[j] * part(heating, j + 1)) for j in wet}
+    push = {j: (gravity * therm_coef) * down_sum(warm[j]) for j in wet}
+    for j in range(2):
+        u, v, t, s = [part(base_ref, j * fields + field) for field in range(fields)]
+        late = wet[j] * part(heating, 4 + j)
+        spread = lap(warm[j - 1], warm[j], warm[j + 1])
+        results = (
+            u + wet[j] * (time_step * slope(push[j])),
+            v + wet[j] * (time_step * (0.5 * (push[j + 1] - push[j - 1]))),
+            t + wet[j] * (warm[j] + time_step * heat_diff * spread) + time_step * late,
+            s,
+        )
+        for field, value in enumerate(results):
+            begin = j * half + field * levels
+            flat[begin : begin + levels, :] = value
     for index in range(half):
         field, level = divmod(index, levels)
-        for row in range(lat_rows):
+        for row in range(2):
             out_ref[field, level, row : row + 1, :] = flat[row * half + index : row * half + index + 1, :]
 
 
@@ -677,6 +772,8 @@
     own = columns // TILE
 
     edge_rows = (species + 1) * (levels * total_lat // LANES) * HALO + 2 * HALO
+    packed_rows = count * 3 * TILE
+    home_shape = (LANES + TILE, total_lon)
     kinds = rate_table.shape[0]
     roomy = pltpu.CompilerParams(vmem_limit_bytes=GRANT)
     ocean_state, bottom, tracers, land_sea, biome_id, rate_table = placed(
@@ -690,25 +787,28 @@
     sizes = (levels, species, total_lat, columns, kinds)
     edge_shape = (species, levels, TILE, total_lat)
 
-    packed, to_first, to_second = pl.pallas_call(
+    packed, to_first, to_second, home = pl.pallas_call(
         pack,
-        out_shape=[far(count * (own + 1) * TILE, LANES), near(edge_rows, LANES), near(edge_rows, LANES)],
+        out_shape=[far(packed_rows, LANES), near(edge_rows, LANES), near(edge_rows, LANES), far(*home_shape)],
         in_specs=[hbm] * 5,
-        out_specs=[hbm, vmem, vmem],
-        scratch_shapes=grids((LANES, total_lon), (TILE, total_lon), ocean_state.shape)
+        out_specs=[hbm, vmem, vmem, hbm],
+        scratch_shapes=grids((total_lon, LANES), (6 * (total_lon // TILE + 2 * TILE), LANES), ocean_state.shape)
         + [pltpu.VMEM(bottom.shape, bottom.dtype)]
         + grids(edge_shape, edge_shape)
         + [pltpu.VMEM(x.shape, x.dtype) for x in (land_sea, biome_id)]
-        + grids((count * (own + 1) * TILE, LANES))
-        + [pltpu.SemaphoreType.DMA((6,)), pltpu.SemaphoreType.DMA],
+        + grids((packed_rows, LANES), home_shape)
+        + [pltpu.SemaphoreType.DMA((6,)), pltpu.SemaphoreType.DMA((2,))],
         compiler_params=roomy,
         name="pack",
     )(ocean_state, bottom, tracers, land_sea, biome_id)
     received = lax.all_to_all(
-        packed.reshape(count, (own + 1) * TILE, LANES), "lat", split_axis=0, concat_axis=0, tiled=True
+        packed.reshape(count, packed_rows // count, LANES), "lat", split_axis=0, concat_axis=0, tiled=True
     ).reshape(packed.shape)
     from_first = lax.ppermute(to_first, "lat", pairs)
     from_second = lax.ppermute(to_second, "lat", others)
+    first_rows = lax.ppermute(home, "lat", pairs)
+    inner = [(a, b) for a, b in others if abs(a - b) == 1]
+    second_rows = lax.ppermute(home, "lat", inner)
     from_first, from_second, received = placed(pltpu.VMEM, from_first, from_second, received)
 
     inside = pl.pallas_call(
@@ -751,11 +851,12 @@
         out_specs=[hbm, vmem],
         scratch_shapes=grids(
             (count * own * TILE, LANES),
-            (4 * LANES, LANES),
-            (FIELDS * cells, LANES),
+            (TILE * LANES, LANES),
+            (3 * cells, LANES),
             (STEPS * 7 * cells, LANES),
             (2 * size, LANES),
             (cells, LANES),
+            (6 * cells, LANES),
         )
         + [pltpu.SemaphoreType.DMA],
         compiler_params=pltpu.CompilerParams(vmem_limit_bytes=GRANT),
@@ -764,6 +865,18 @@
     back = lax.all_to_all(
         sent.reshape(count, own * TILE, LANES), "lat", split_axis=0, concat_axis=0, tiled=True
     ).reshape(sent.shape)
+
+    def stay(*refs):
+        at_home(*refs, levels, total_lat)
+
+    base, masks = pl.pallas_call(
+        stay,
+        out_shape=[near(LANES, total_lon), near(4 * levels, total_lon)],
+        in_specs=[vmem] * 3,
+        out_specs=[vmem] * 2,
+        compiler_params=roomy,
+        name="at_home",
+    )(*placed(pltpu.HBM, home, first_rows, second_rows))
     (back,) = placed(pltpu.VMEM, back)
     (last,) = placed(pltpu.VMEM, last)
     tracers_out = pl.pallas_call(
@@ -775,14 +888,14 @@
         name="unpack_tracers",
     )(last)
     state_out = pl.pallas_call(
-        unpack_ocean,
+        finish,
         out_shape=far(*ocean_state.shape),
-        in_specs=[vmem],
+        in_specs=[vmem] * 3,
         out_specs=vmem,
-        scratch_shapes=grids((total_lon, LANES), (LANES, total_lon)),
+        scratch_shapes=grids((LANES, total_lon)),
         compiler_params=roomy,
-        name="unpack_ocean",
-    )(back)
+        name="finish",
+    )(back, base, masks)
     return (state_out, tracers_out)
 
 

time: 43.9 us -> 48.6 us (1.11)
  the two profiles are of different devices: /device:TPU:0 before, /device:TPU:9 now
where the time goes in v4:
time: 48.6 us; the launch traced here: 48.3 us
  Pallas kernels  18 us (37%)
  starting transfers between devices  17.7 us (36%)
  waiting for transfers between devices  10.4 us (21%)
  local copies, waits for them, and re-layouts  1.36 us (3%)
  between operations  0.7 us (1%)
    ppermute x1, waiting for transfers between devices, shards(): second_rows = lax.ppermute(home, 'lat', inner)  6.79 us
    pallas_call x1, Pallas kernels, shards(): pl.pallas_call(run, out_shape=[far(count * own * TILE, LANES), near(size,...  6.78 us
    all_to_all x1, starting transfers between devices, shards(): lax.all_to_all(packed.reshape(count, packed_rows // count, LANES), 'lat',...  6.59 us
    all_to_all x1, starting transfers between devices, shards(): lax.all_to_all(sent.reshape(count, own * TILE, LANES), 'lat', split_axis=...  6.05 us
    ppermute x1, waiting for transfers between devices, shards(): from_second = lax.ppermute(to_second, 'lat', others)  3.65 us
    ppermute x1, starting transfers between devices, shards(): second_rows = lax.ppermute(home, 'lat', inner)  3.37 us
    pallas_call x1, Pallas kernels, shards(): pl.pallas_call(prepare_own, out_shape=[near(size, LANES), near(cells, LAN...  2.64 us
    pallas_call x1, Pallas kernels, shards(): pl.pallas_call(pack, out_shape=[far(packed_rows, LANES), near(edge_rows,...  2.41 us
  transfers between devices with their start and end apart: 6, of which 2 were waited for; matrix products, arithmetic and copies ran while one was open for 0% of the time, Pallas kernels for 16%

profile of v4, /device:TPU:9, one launch (start us, length us, event | category | flops | bytes accessed | tf_op | source)
XLA Modules:
  0.0 48.3 jit_solution(4379555498367297855)
XLA Ops:
  0.6 2.4 %pack.1 = (f32[384,128]{1,0:T(8,128)}, f32[280,128]{1,0:T(8,128)S(1)}, f32[280,128]{1,0:T(8,128)S(1)}, f32[136,384]{1,0:T(8,128)}) custom-call(f32[4,16,2,384]{3,2,1,0:T(2,128)} %ocean.1, s32[2,384]{1,0:T(2,128)} %bottom.1, f32[16,16,24,32]{3,2,1,0:T(8,128)} %tracers.3, s32[16,24,32]{2,1,0:T(8,128)} %sea.3, s32[24,32]{1,0:T(8,128)} %biome.3), custom_call_target="tpu_custom_call" | custom-call | tf_op jit(solution)/shard_map/pack/pallas_call | solution.py:790
  3.0 6.6 %all-to-all-start = ((f32[16,24,128]{2,1,0:T(8,128)}), f32[16,24,128]{2,1,0:T(8,128)S(1)}, u32[]{:S(2)}, u32[]{:S(2)}) async-start(f32[16,24,128]{2,1,0:T(8,128)} %bitcast.6), calls=%async_computation | async-start | bytes 393216 | tf_op jit(solution)/shard_map/all_to_all | solution.py:804
  9.6 0.4 collective-permute-start
  10.0 1.2 %collective-permute-start.1 = (f32[280,128]{1,0:T(8,128)S(1)}, f32[280,128]{1,0:T(8,128)S(1)}, u32[]{:S(2)}, u32[]{:S(2)}) collective-permute-start(f32[280,128]{1,0:T(8,128)S(1)} %get-tuple-element.24), channel_id=1, source_target_pairs={{1,2},{2,1},{3,4},{4,3},{5,6},{6,5},{7,8},{8,7},{9,10},{10,9},{11,... | collective-permute-start | bytes 430088 | tf_op jit(solution)/shard_map/ppermute | solution.py:808
  11.2 2.6 %prepare_own.1 = (f32[2048,128]{1,0:T(8,128)S(1)}, f32[128,128]{1,0:T(8,128)S(1)}, f32[8,128]{1,0:T(8,128)S(1)}, bf16[64,48]{1,0:T(8,128)(2,1)S(1)}) custom-call(f32[16,16,24,32]{3,2,1,0:T(8,128)} %tracers.3, s32[16,24,32]{2,1,0:T(8,128)} %sea.3, s32[24,32]{1,0:T(8,128)} %biome.3, f32[4,16,16]{2,1,0:T(8,128)} %rate_table.1), custom_call_target="tpu_custom_call" | custom-call | tf_op jit(solution)/shard_map/prepare_own/pallas_call | solution.py:814
  13.9 0.0 collective-permute-done.refs_4_
  13.9 3.6 %collective-permute-done.1.refs_5_ = f32[280,128]{1,0:T(8,128)S(1)} collective-permute-done((f32[280,128]{1,0:T(8,128)S(1)}, f32[280,128]{1,0:T(8,128)S(1)}, u32[]{:S(2)}, u32[]{:S(2)}) %collective-permute-start.1) | collective-permute-done | bytes 143392 | tf_op jit(solution)/shard_map/ppermute | solution.py:808
  17.5 1.3 %prepare.1 = (f32[2048,128]{1,0:T(8,128)S(1)}, f32[128,128]{1,0:T(8,128)S(1)}, f32[8,128]{1,0:T(8,128)S(1)}, f32[2048,128]{1,0:T(8,128)S(1)}) custom-call(f32[2048,128]{1,0:T(8,128)S(1)} %get-tuple-element.19.refs_0_, f32[128,128]{1,0:T(8,128)S(1)} %get-tuple-element.20.refs_1_, f32[8,128]{1,0:T(8,128)S(1)} %get-tuple-element.21.refs_2_, ...), custom_call_target="tpu_custom_call" | custom-call | tf_op jit(solution)/shard_map/prepare/pallas_call | solution.py:834
  18.9 0.0 all-to-all-done
  18.9 6.8 %advance.1 = (f32[384,128]{1,0:T(8,128)}, f32[2048,128]{1,0:T(8,128)S(1)}) custom-call(f32[384,128]{1,0:T(8,128)S(1)} %bitcast.4, f32[2048,128]{1,0:T(8,128)S(1)} %get-tuple-element.25.refs_1_, f32[128,128]{1,0:T(8,128)S(1)} %get-tuple-element.26.refs_2_, f32[8,128]{1,0:T(8,128)S(1)} %get-tuple-element.27.refs_3_, ...), custom_call_target="tpu_custom_call" | custom-call | tf_op jit(solution)/shard_map/advance/pallas_call | solution.py:847
  25.7 6.1 %all-to-all-start.1 = ((f32[16,24,128]{2,1,0:T(8,128)}), f32[16,24,128]{2,1,0:T(8,128)S(1)}, u32[]{:S(2)}, u32[]{:S(2)}) async-start(f32[16,24,128]{2,1,0:T(8,128)} %bitcast.7), calls=%async_computation.1 | async-start | bytes 393216 | tf_op jit(solution)/shard_map/all_to_all | solution.py:865
  31.7 3.4 %collective-permute-start.3 = (f32[136,384]{1,0:T(8,128)}, f32[136,384]{1,0:T(8,128)S(1)}, u32[]{:S(2)}, u32[]{:S(2)}) collective-permute-start(f32[136,384]{1,0:T(8,128)} %get-tuple-element.30.refs_0_), channel_id=1, source_target_pairs={{1,2},{2,1},{3,4},{4,3},{5,6},{6,5},{7,8},{8,7},{9,10},{10,9},{11,... | collective-permute-start | bytes 626696 | tf_op jit(solution)/shard_map/ppermute | solution.py:811
  35.1 0.2 collective-permute-start.2
  35.2 6.8 %collective-permute-done.3.refs_2_ = f32[136,384]{1,0:T(8,128)S(1)} collective-permute-done((f32[136,384]{1,0:T(8,128)}, f32[136,384]{1,0:T(8,128)S(1)}, u32[]{:S(2)}, u32[]{:S(2)}) %collective-permute-start.3) | collective-permute-done | bytes 208928 | tf_op jit(solution)/shard_map/ppermute | solution.py:811
  42.0 0.0 copy-start
  42.0 0.0 collective-permute-done.2.refs_1_
  42.0 0.7 %copy-done = f32[136,384]{1,0:T(8,128)} copy-done((f32[136,384]{1,0:T(8,128)}, f32[136,384]{1,0:T(8,128)S(1)}, u32[]{:S(2)}) %copy-start) | copy-done | bytes 208920
  42.7 0.0 copy-start.1
  42.7 0.7 %copy-done.1 = f32[136,384]{1,0:T(8,128)} copy-done((f32[136,384]{1,0:T(8,128)}, f32[136,384]{1,0:T(8,128)S(1)}, u32[]{:S(2)}) %copy-start.1) | copy-done | bytes 208920
  43.4 1.6 %at_home.1 = (f32[128,384]{1,0:T(8,128)S(1)}, f32[64,384]{1,0:T(8,128)S(1)}) custom-call(f32[136,384]{1,0:T(8,128)} %get-tuple-element.30.refs_0_, f32[136,384]{1,0:T(8,128)} %copy-done.1, f32[136,384]{1,0:T(8,128)} %copy-done), custom_call_target="tpu_custom_call" | custom-call | tf_op jit(solution)/shard_map/at_home/pallas_call | solution.py:872
  45.0 2.3 %unpack_tracers.1 = f32[16,16,24,32]{3,2,1,0:T(8,128)} custom-call(f32[2048,128]{1,0:T(8,128)S(1)} %get-tuple-element.33.last_ref), custom_call_target="tpu_custom_call" | custom-call | tf_op jit(solution)/shard_map/unpack_tracers/pallas_call | solution.py:882
  47.3 0.0 all-to-all-done.1
  47.3 1.0 %finish.1 = f32[4,16,2,384]{3,2,1,0:T(2,128)} custom-call(f32[384,128]{1,0:T(8,128)S(1)} %bitcast.5, f32[128,384]{1,0:T(8,128)S(1)} %get-tuple-element.31.base_ref, f32[64,384]{1,0:T(8,128)S(1)} %get-tuple-element.32.wet_ref), custom_call_target="tpu_custom_call" | custom-call | tf_op jit(solution)/shard_map/finish/pallas_call | solution.py:890
Async XLA Ops:
  3.0 15.8 %all-to-all-start = ((f32[16,24,128]{2,1,0:T(8,128)}), f32[16,24,128]{2,1,0:T(8,128)S(1)}, u32[]{:S(2)}, u32[]{:S(2)}) async-start(f32[16,24,128]{2,1,0:T(8,128)} %bitcast.6), calls=%async_computation | async-start | bytes 393216 | tf_op jit(solution)/shard_map/all_to_all | solution.py:804
  9.6 4.2 %collective-permute-start = (f32[280,128]{1,0:T(8,128)S(1)}, f32[280,128]{1,0:T(8,128)S(1)}, u32[]{:S(2)}, u32[]{:S(2)}) collective-permute-start(f32[280,128]{1,0:T(8,128)S(1)} %get-tuple-element.23), channel_id=1, source_target_pairs={{0,1},{1,0},{2,3},{3,2},{4,5},{5,4},{6,7},{7,6},{8,9},{9,8},{10,11... | collective-permute-start | bytes 430088 | tf_op jit(solution)/shard_map/ppermute | solution.py:807
  10.0 7.5 %collective-permute-start.1 = (f32[280,128]{1,0:T(8,128)S(1)}, f32[280,128]{1,0:T(8,128)S(1)}, u32[]{:S(2)}, u32[]{:S(2)}) collective-permute-start(f32[280,128]{1,0:T(8,128)S(1)} %get-tuple-element.24), channel_id=1, source_target_pairs={{1,2},{2,1},{3,4},{4,3},{5,6},{6,5},{7,8},{8,7},{9,10},{10,9},{11,... | collective-permute-start | bytes 430088 | tf_op jit(solution)/shard_map/ppermute | solution.py:808
  25.7 21.6 %all-to-all-start.1 = ((f32[16,24,128]{2,1,0:T(8,128)}), f32[16,24,128]{2,1,0:T(8,128)S(1)}, u32[]{:S(2)}, u32[]{:S(2)}) async-start(f32[16,24,128]{2,1,0:T(8,128)} %bitcast.7), calls=%async_computation.1 | async-start | bytes 393216 | tf_op jit(solution)/shard_map/all_to_all | solution.py:865
  31.7 10.3 %collective-permute-start.3 = (f32[136,384]{1,0:T(8,128)}, f32[136,384]{1,0:T(8,128)S(1)}, u32[]{:S(2)}, u32[]{:S(2)}) collective-permute-start(f32[136,384]{1,0:T(8,128)} %get-tuple-element.30.refs_0_), channel_id=1, source_target_pairs={{1,2},{2,1},{3,4},{4,3},{5,6},{6,5},{7,8},{8,7},{9,10},{10,9},{11,... | collective-permute-start | bytes 626696 | tf_op jit(solution)/shard_map/ppermute | solution.py:811
  35.1 7.0 %collective-permute-start.2 = (f32[136,384]{1,0:T(8,128)}, f32[136,384]{1,0:T(8,128)S(1)}, u32[]{:S(2)}, u32[]{:S(2)}) collective-permute-start(f32[136,384]{1,0:T(8,128)} %get-tuple-element.30.refs_0_), channel_id=1, source_target_pairs={{0,1},{1,0},{2,3},{3,2},{4,5},{5,4},{6,7},{7,6},{8,9},{9,8},{10,11... | collective-permute-start | bytes 626696 | tf_op jit(solution)/shard_map/ppermute | solution.py:809
  42.0 0.7 %copy-start = (f32[136,384]{1,0:T(8,128)}, f32[136,384]{1,0:T(8,128)S(1)}, u32[]{:S(2)}) copy-start(f32[136,384]{1,0:T(8,128)S(1)} %collective-permute-done.3.refs_2_) | copy-start | bytes 626692
  42.7 0.7 %copy-start.1 = (f32[136,384]{1,0:T(8,128)}, f32[136,384]{1,0:T(8,128)S(1)}, u32[]{:S(2)}) copy-start(f32[136,384]{1,0:T(8,128)S(1)} %collective-permute-done.2.refs_1_) | copy-start | bytes 626692

commit v5 on v4

--- a/solution.py
+++ b/solution.py
@@ -633,16 +633,17 @@
                 at = ((place + 4 * step) * levels + k) * TILE
                 heat[at : at + TILE, :] = spin(heating, -shift, 1)
 
-    kinds_of_row = 6 * levels
-    blank = jnp.zeros((LANES - kinds_of_row, LANES), jnp.float32)
-    for r in range(TILE):
-        work[r * LANES : (r + 1) * LANES, :] = jnp.concatenate(
-            [heat[pl.ds(r, kinds_of_row, stride=TILE), :], blank], axis=0
-        ).T
+    each = own * 6
+    early, late = 4 * levels, 2 * levels
+    for block in range(6):
+        if block < 4:
+            parts = [heat[pl.ds(2 * block + i, early, stride=TILE), :] for i in range(2)]
+        else:
+            parts = [heat[pl.ds(early * TILE + 4 * (block - 4) + i, late, stride=TILE), :] for i in range(4)]
+        work[block * LANES : (block + 1) * LANES, :] = jnp.concatenate(parts, axis=0).T
         for q in range(own):
-            sent[pl.ds(q * TILE + r, count, stride=own * TILE), :] = work[
-                pl.ds(r * LANES + q * total_lat, count, stride=2), :
-            ]
+            place = q * 4 + block if block < 4 else own * 4 + q * 2 + block - 4
+            sent[pl.ds(place, count, stride=each), :] = work[pl.ds(block * LANES + q * total_lat, count, stride=2), :]
     send = pltpu.make_async_copy(sent, sent_out, done)
     send.start()
     send.wait()
@@ -715,10 +716,22 @@
         wet_ref[(j + 1) * levels : (j + 2) * levels, :] = wet[j]
 
 
-def finish(received, base_ref, wet_ref, out_ref, flat):
+def finish(received, base_ref, wet_ref, out_ref, early, late, flat):
     fields, levels, _, _ = out_ref.shape
     half = fields * levels
-    heating = received[...].T
+    columns = 3 * TILE
+    count = out_ref.shape[3] // columns
+    each = received.shape[0] // count
+    for place in range(each):
+        line = received[pl.ds(place, count, stride=each), :]
+        if place < columns // 2:
+            for i in range(2):
+                early[pl.ds(2 * place + i, count, stride=columns), :] = spin(line, -i * LANES // 2, 1)
+        else:
+            for i in range(4):
+                begin = 4 * (place - columns // 2) + i
+                late[pl.ds(begin, count, stride=columns), :] = spin(line, (2 - i) * LANES // 4, 1)
+    heating = jnp.where(lanes_of(early.shape) < LANES // 2, early[...], late[...]).T
 
     def part(ref, place):
         return ref[place * levels : (place + 1) * levels, :]
@@ -846,11 +859,11 @@
 
     sent, last = pl.pallas_call(
         run,
-        out_shape=[far(count * own * TILE, LANES), near(size, LANES)],
+        out_shape=[far(count * own * 6, LANES), near(size, LANES)],
         in_specs=[vmem] * 6,
         out_specs=[hbm, vmem],
         scratch_shapes=grids(
-            (count * own * TILE, LANES),
+            (count * own * 6, LANES),
             (TILE * LANES, LANES),
             (3 * cells, LANES),
             (STEPS * 7 * cells, LANES),
@@ -863,7 +876,7 @@
         name="advance",
     )(received, now, wet, biomes, pieces, first)
     back = lax.all_to_all(
-        sent.reshape(count, own * TILE, LANES), "lat", split_axis=0, concat_axis=0, tiled=True
+        sent.reshape(count, 1, own * 6 * LANES), "lat", split_axis=0, concat_axis=0, tiled=True
     ).reshape(sent.shape)
 
     def stay(*refs):
@@ -892,7 +905,7 @@
         out_shape=far(*ocean_state.shape),
         in_specs=[vmem] * 3,
         out_specs=vmem,
-        scratch_shapes=grids((LANES, total_lon)),
+        scratch_shapes=grids((total_lon, LANES), (total_lon, LANES), (LANES, total_lon)),
         compiler_params=roomy,
         name="finish",
     )(back, base, masks)

time: 48.6 us -> 48.3 us (level)
  the two profiles are of different devices: /device:TPU:9 before, /device:TPU:1 now
where the time goes in v5:
time: 48.3 us; the launch traced here: 47.9 us
  starting transfers between devices  19.5 us (40%)
  Pallas kernels  18.1 us (37%)
  waiting for transfers between devices  8.35 us (17%)
  local copies, waits for them, and re-layouts  1.35 us (3%)
  between operations  0.7 us (1%)
    all_to_all x1, starting transfers between devices, shards(): lax.all_to_all(packed.reshape(count, packed_rows // count, LANES), 'lat',...  7.35 us
    all_to_all x1, starting transfers between devices, shards(): lax.all_to_all(sent.reshape(count, 1, own * 6 * LANES), 'lat', split_axis...  6.78 us
    pallas_call x1, Pallas kernels, shards(): pl.pallas_call(run, out_shape=[far(count * own * 6, LANES), near(size, LA...  6.68 us
    ppermute x1, waiting for transfers between devices, shards(): second_rows = lax.ppermute(home, 'lat', inner)  5.6 us
    ppermute x1, starting transfers between devices, shards(): second_rows = lax.ppermute(home, 'lat', inner)  3.53 us
    pallas_call x1, Pallas kernels, shards(): pl.pallas_call(prepare_own, out_shape=[near(size, LANES), near(cells, LAN...  2.64 us
    pallas_call x1, Pallas kernels, shards(): pl.pallas_call(pack, out_shape=[far(packed_rows, LANES), near(edge_rows,...  2.41 us
    pallas_call x1, Pallas kernels, shards(): pl.pallas_call(unpack_tracers, out_shape=far(*tracers.shape), in_specs=[v...  2.28 us
  transfers between devices with their start and end apart: 6, of which 3 were waited for; matrix products, arithmetic and copies ran while one was open for 0% of the time, Pallas kernels for 16%

profile of v5, /device:TPU:1, one launch (start us, length us, event | category | flops | bytes accessed | tf_op | source)
XLA Modules:
  0.0 47.9 jit_solution(2284642200051151359)
XLA Ops:
  0.6 2.4 %pack.1 = (f32[384,128]{1,0:T(8,128)}, f32[280,128]{1,0:T(8,128)S(1)}, f32[280,128]{1,0:T(8,128)S(1)}, f32[136,384]{1,0:T(8,128)}) custom-call(f32[4,16,2,384]{3,2,1,0:T(2,128)} %ocean.1, s32[2,384]{1,0:T(2,128)} %bottom.1, f32[16,16,24,32]{3,2,1,0:T(8,128)} %tracers.3, s32[16,24,32]{2,1,0:T(8,128)} %sea.3, s32[24,32]{1,0:T(8,128)} %biome.3), custom_call_target="tpu_custom_call" | custom-call | tf_op jit(solution)/shard_map/pack/pallas_call | solution.py:803
  3.0 7.4 %all-to-all-start = ((f32[16,24,128]{2,1,0:T(8,128)}), f32[16,24,128]{2,1,0:T(8,128)S(1)}, u32[]{:S(2)}, u32[]{:S(2)}) async-start(f32[16,24,128]{2,1,0:T(8,128)} %bitcast.6), calls=%async_computation | async-start | bytes 393216 | tf_op jit(solution)/shard_map/all_to_all | solution.py:817
  10.4 0.2 collective-permute-start
  10.6 1.6 %collective-permute-start.1 = (f32[280,128]{1,0:T(8,128)S(1)}, f32[280,128]{1,0:T(8,128)S(1)}, u32[]{:S(2)}, u32[]{:S(2)}) collective-permute-start(f32[280,128]{1,0:T(8,128)S(1)} %get-tuple-element.24), channel_id=1, source_target_pairs={{1,2},{2,1},{3,4},{4,3},{5,6},{6,5},{7,8},{8,7},{9,10},{10,9},{11,... | collective-permute-start | bytes 430088 | tf_op jit(solution)/shard_map/ppermute | solution.py:821
  12.1 2.6 %prepare_own.1 = (f32[2048,128]{1,0:T(8,128)S(1)}, f32[128,128]{1,0:T(8,128)S(1)}, f32[8,128]{1,0:T(8,128)S(1)}, bf16[64,48]{1,0:T(8,128)(2,1)S(1)}) custom-call(f32[16,16,24,32]{3,2,1,0:T(8,128)} %tracers.3, s32[16,24,32]{2,1,0:T(8,128)} %sea.3, s32[24,32]{1,0:T(8,128)} %biome.3, f32[4,16,16]{2,1,0:T(8,128)} %rate_table.1), custom_call_target="tpu_custom_call" | custom-call | tf_op jit(solution)/shard_map/prepare_own/pallas_call | solution.py:827
  14.8 0.0 collective-permute-done.refs_4_
  14.8 1.9 %collective-permute-done.1.refs_5_ = f32[280,128]{1,0:T(8,128)S(1)} collective-permute-done((f32[280,128]{1,0:T(8,128)S(1)}, f32[280,128]{1,0:T(8,128)S(1)}, u32[]{:S(2)}, u32[]{:S(2)}) %collective-permute-start.1) | collective-permute-done | bytes 143392 | tf_op jit(solution)/shard_map/ppermute | solution.py:821
  16.7 1.3 %prepare.1 = (f32[2048,128]{1,0:T(8,128)S(1)}, f32[128,128]{1,0:T(8,128)S(1)}, f32[8,128]{1,0:T(8,128)S(1)}, f32[2048,128]{1,0:T(8,128)S(1)}) custom-call(f32[2048,128]{1,0:T(8,128)S(1)} %get-tuple-element.19.refs_0_, f32[128,128]{1,0:T(8,128)S(1)} %get-tuple-element.20.refs_1_, f32[8,128]{1,0:T(8,128)S(1)} %get-tuple-element.21.refs_2_, ...), custom_call_target="tpu_custom_call" | custom-call | tf_op jit(solution)/shard_map/prepare/pallas_call | solution.py:847
  18.0 0.8 %all-to-all-done = f32[16,24,128]{2,1,0:T(8,128)S(1)} async-done(((f32[16,24,128]{2,1,0:T(8,128)}), f32[16,24,128]{2,1,0:T(8,128)S(1)}, u32[]{:S(2)}, u32[]{:S(2)}) %all-to-all-start) | async-done | bytes 196640 | tf_op jit(solution)/shard_map/all_to_all | solution.py:817
  18.9 6.7 %advance.1 = (f32[288,128]{1,0:T(8,128)}, f32[2048,128]{1,0:T(8,128)S(1)}) custom-call(f32[384,128]{1,0:T(8,128)S(1)} %bitcast.4, f32[2048,128]{1,0:T(8,128)S(1)} %get-tuple-element.25.refs_1_, f32[128,128]{1,0:T(8,128)S(1)} %get-tuple-element.26.refs_2_, f32[8,128]{1,0:T(8,128)S(1)} %get-tuple-element.27.refs_3_, ...), custom_call_target="tpu_custom_call" | custom-call | tf_op jit(solution)/shard_map/advance/pallas_call | solution.py:860
  25.6 6.8 %all-to-all-start.1 = ((f32[16,1,2304]{2,1,0:T(1,128)}), f32[16,1,2304]{2,1,0:T(1,128)S(1)}, u32[]{:S(2)}, u32[]{:S(2)}) async-start(f32[16,1,2304]{2,1,0:T(1,128)} %bitcast.7), calls=%async_computation.1 | async-start | bytes 294912 | tf_op jit(solution)/shard_map/all_to_all | solution.py:878
  32.3 3.5 %collective-permute-start.3 = (f32[136,384]{1,0:T(8,128)}, f32[136,384]{1,0:T(8,128)S(1)}, u32[]{:S(2)}, u32[]{:S(2)}) collective-permute-start(f32[136,384]{1,0:T(8,128)} %get-tuple-element.30.refs_0_), channel_id=1, source_target_pairs={{1,2},{2,1},{3,4},{4,3},{5,6},{6,5},{7,8},{8,7},{9,10},{10,9},{11,... | collective-permute-start | bytes 626696 | tf_op jit(solution)/shard_map/ppermute | solution.py:824
  35.9 0.1 collective-permute-start.2
  36.0 5.6 %collective-permute-done.3.refs_2_ = f32[136,384]{1,0:T(8,128)S(1)} collective-permute-done((f32[136,384]{1,0:T(8,128)}, f32[136,384]{1,0:T(8,128)S(1)}, u32[]{:S(2)}, u32[]{:S(2)}) %collective-permute-start.3) | collective-permute-done | bytes 208928 | tf_op jit(solution)/shard_map/ppermute | solution.py:824
  41.6 0.0 copy-start
  41.6 0.0 collective-permute-done.2.refs_1_
  41.6 0.7 %copy-done = f32[136,384]{1,0:T(8,128)} copy-done((f32[136,384]{1,0:T(8,128)}, f32[136,384]{1,0:T(8,128)S(1)}, u32[]{:S(2)}) %copy-start) | copy-done | bytes 208920
  42.2 0.0 copy-start.1
  42.2 0.7 %copy-done.1 = f32[136,384]{1,0:T(8,128)} copy-done((f32[136,384]{1,0:T(8,128)}, f32[136,384]{1,0:T(8,128)S(1)}, u32[]{:S(2)}) %copy-start.1) | copy-done | bytes 208920
  42.9 1.6 %at_home.1 = (f32[128,384]{1,0:T(8,128)S(1)}, f32[64,384]{1,0:T(8,128)S(1)}) custom-call(f32[136,384]{1,0:T(8,128)} %get-tuple-element.30.refs_0_, f32[136,384]{1,0:T(8,128)} %copy-done.1, f32[136,384]{1,0:T(8,128)} %copy-done), custom_call_target="tpu_custom_call" | custom-call | tf_op jit(solution)/shard_map/at_home/pallas_call | solution.py:885
  44.5 2.3 %unpack_tracers.1 = f32[16,16,24,32]{3,2,1,0:T(8,128)} custom-call(f32[2048,128]{1,0:T(8,128)S(1)} %get-tuple-element.33.last_ref), custom_call_target="tpu_custom_call" | custom-call | tf_op jit(solution)/shard_map/unpack_tracers/pallas_call | solution.py:895
  46.8 0.0 all-to-all-done.1
  46.8 1.1 %finish.1 = f32[4,16,2,384]{3,2,1,0:T(2,128)} custom-call(f32[288,128]{1,0:T(8,128)S(1)} %bitcast.5, f32[128,384]{1,0:T(8,128)S(1)} %get-tuple-element.31.base_ref, f32[64,384]{1,0:T(8,128)S(1)} %get-tuple-element.32.wet_ref), custom_call_target="tpu_custom_call" | custom-call | tf_op jit(solution)/shard_map/finish/pallas_call | solution.py:903
Async XLA Ops:
  3.0 15.8 %all-to-all-start = ((f32[16,24,128]{2,1,0:T(8,128)}), f32[16,24,128]{2,1,0:T(8,128)S(1)}, u32[]{:S(2)}, u32[]{:S(2)}) async-start(f32[16,24,128]{2,1,0:T(8,128)} %bitcast.6), calls=%async_computation | async-start | bytes 393216 | tf_op jit(solution)/shard_map/all_to_all | solution.py:817
  10.4 4.4 %collective-permute-start = (f32[280,128]{1,0:T(8,128)S(1)}, f32[280,128]{1,0:T(8,128)S(1)}, u32[]{:S(2)}, u32[]{:S(2)}) collective-permute-start(f32[280,128]{1,0:T(8,128)S(1)} %get-tuple-element.23), channel_id=1, source_target_pairs={{0,1},{1,0},{2,3},{3,2},{4,5},{5,4},{6,7},{7,6},{8,9},{9,8},{10,11... | collective-permute-start | bytes 430088 | tf_op jit(solution)/shard_map/ppermute | solution.py:820
  10.6 6.1 %collective-permute-start.1 = (f32[280,128]{1,0:T(8,128)S(1)}, f32[280,128]{1,0:T(8,128)S(1)}, u32[]{:S(2)}, u32[]{:S(2)}) collective-permute-start(f32[280,128]{1,0:T(8,128)S(1)} %get-tuple-element.24), channel_id=1, source_target_pairs={{1,2},{2,1},{3,4},{4,3},{5,6},{6,5},{7,8},{8,7},{9,10},{10,9},{11,... | collective-permute-start | bytes 430088 | tf_op jit(solution)/shard_map/ppermute | solution.py:821
  25.6 21.3 %all-to-all-start.1 = ((f32[16,1,2304]{2,1,0:T(1,128)}), f32[16,1,2304]{2,1,0:T(1,128)S(1)}, u32[]{:S(2)}, u32[]{:S(2)}) async-start(f32[16,1,2304]{2,1,0:T(1,128)} %bitcast.7), calls=%async_computation.1 | async-start | bytes 294912 | tf_op jit(solution)/shard_map/all_to_all | solution.py:878
  32.3 9.2 %collective-permute-start.3 = (f32[136,384]{1,0:T(8,128)}, f32[136,384]{1,0:T(8,128)S(1)}, u32[]{:S(2)}, u32[]{:S(2)}) collective-permute-start(f32[136,384]{1,0:T(8,128)} %get-tuple-element.30.refs_0_), channel_id=1, source_target_pairs={{1,2},{2,1},{3,4},{4,3},{5,6},{6,5},{7,8},{8,7},{9,10},{10,9},{11,... | collective-permute-start | bytes 626696 | tf_op jit(solution)/shard_map/ppermute | solution.py:824
  35.9 5.7 %collective-permute-start.2 = (f32[136,384]{1,0:T(8,128)}, f32[136,384]{1,0:T(8,128)S(1)}, u32[]{:S(2)}, u32[]{:S(2)}) collective-permute-start(f32[136,384]{1,0:T(8,128)} %get-tuple-element.30.refs_0_), channel_id=1, source_target_pairs={{0,1},{1,0},{2,3},{3,2},{4,5},{5,4},{6,7},{7,6},{8,9},{9,8},{10,11... | collective-permute-start | bytes 626696 | tf_op jit(solution)/shard_map/ppermute | solution.py:822
  41.6 0.7 %copy-start = (f32[136,384]{1,0:T(8,128)}, f32[136,384]{1,0:T(8,128)S(1)}, u32[]{:S(2)}) copy-start(f32[136,384]{1,0:T(8,128)S(1)} %collective-permute-done.3.refs_2_) | copy-start | bytes 626692
  42.2 0.7 %copy-start.1 = (f32[136,384]{1,0:T(8,128)}, f32[136,384]{1,0:T(8,128)S(1)}, u32[]{:S(2)}) copy-start(f32[136,384]{1,0:T(8,128)S(1)} %collective-permute-done.2.refs_1_) | copy-start | bytes 626692
